TPU v7x, 32 devices: a whole 2x2x4 slice. The times are simulated.
32 devices in a mesh: req: 8 (over z, y), head: 4 (over x, core).
Axes of the slice: x: 2, y: 2, z: 4, core: 2. Of those that a mesh axis runs over, the one named last changes fastest.
Arguments:
- stream_in: bfloat16 [512, 2560], P('req'), may hold values from -6 to 6
- norm_gain: float32 [2560], replicated, may hold values from 0.25 to 1.75
- gate_weight: bfloat16 [2560, 5120], P(None, 'head'), may hold values from -0.125 to 0.125
- inner_weight: bfloat16 [2560, 5120], P(None, 'head'), may hold values from -0.125 to 0.125
- readwrite_weight: bfloat16 [2560, 256], replicated, may hold values from -0.125 to 0.125
- step_weight: bfloat16 [2560, 80], P(None, 'head'), may hold values from -0.125 to 0.125
- conv_inner: bfloat16 [4, 5120], P(None, 'head'), may hold values from -3 to 3
- conv_readwrite: bfloat16 [4, 256], replicated, may hold values from -3 to 3
- decay_log: float32 [80], P('head'), may hold values from 0 to 2.77
- step_bias: float32 [80], P('head'), may hold values from -4 to -1
- skip_gain: float32 [80], P('head'), may hold values from 0.5 to 1.5
- gate_gain: float32 [5120], P('head'), may hold values from 0.25 to 1.75
- out_weight: bfloat16 [5120, 2560], P('head'), may hold values from -0.078125 to 0.078125
- final_gain: float32 [2560], replicated, may hold values from 0.25 to 1.75
- embedding: bfloat16 [50304, 2560], P(('req', 'head')), may hold values from -0.375 to 0.375
- state_cache: bfloat16 [128, 80, 64, 128], P('req', 'head'), may hold values from -4 to 4
- window_inner: bfloat16 [128, 3, 5120], P('req', None, 'head'), may hold values from -6 to 6
- window_readwrite: bfloat16 [128, 3, 256], P('req'), may hold values from -6 to 6
- source_row: int32 [128], replicated, may hold values from 0 to 127, as said below
- lengths: int32 [128], P('req'), may hold values from 1 to 4, 320 in all
- draft_ids: int32 [512], replicated, may hold values from 0 to 50303
Outputs:
- state_after: bfloat16 [128, 80, 64, 128], P('req', 'head')
- tail_inner: bfloat16 [128, 3, 5120], P('req', None, 'head')
- tail_readwrite: bfloat16 [128, 3, 256], P('req')
- hidden_rms: float32 [512], P(('req', 'head'))
- top_logit: float32 [512], P(('req', 'head'))
- draft_logit: float32 [512], P(('req', 'head'))
Inputs may be any that keep to these rules, and one draw needn't show every extreme that they name: `source_row`: a permutation of the requests; of the 16 requests r * 16 to r * 16 + 15, exactly 2 have their stored row in each block of 16 rows. The first lengths[r] slots of request r are live.
All inputs are finite; a program needn't handle non-finite values. No bound on the sum of `lengths` on one device may be relied on, other than what follows from the above.
Results may differ from a plain program's by a relative error of at most 0.01.
Values may be sent and summed in bfloat16 or wider, within the bound.
No kernel may reach another device: no remote copies, remote signals or barrier semaphores. Data moves between devices by JAX's collectives and lax.ppermute only.
A program may use at most 320 MiB of HBM per device.

v0:
```python
import jax
import jax.numpy as jnp
from jax import lax
from jax.sharding import PartitionSpec as P

epsilon = 1e-05
lowest = -1e30


def rms_of(values):
    return jnp.sqrt(jnp.mean(values * values, axis=-1, keepdims=True) + epsilon)


def conv_silu(window, weight):
    taps = weight.shape[0]
    count = window.shape[1] - taps + 1
    total = jnp.zeros((window.shape[0], count, window.shape[2]), jnp.float32)
    for kernel_tap in range(taps):
        total = total + window[:, kernel_tap : kernel_tap + count].astype(jnp.float32) * weight[
            kernel_tap
        ].astype(jnp.float32)
    return jax.nn.silu(total).astype(jnp.bfloat16)


def last_rows(window, lengths, keep):
    places = jnp.arange(window.shape[1], dtype=jnp.int32)
    wide = window.astype(jnp.float32)
    picked = []
    for lag_index in range(keep):
        select = (places[None, :] == lengths[:, None] + lag_index).astype(jnp.float32)
        picked.append(jnp.sum(select[:, :, None] * wide, axis=1))
    return jnp.stack(picked, axis=1).astype(jnp.bfloat16)


def run_slots(state, inner, writes, reads, steps, decays, skip_gain):
    outputs = []
    for slot_index in range(inner.shape[1]):
        current = inner[:, slot_index].astype(jnp.float32)
        update = (steps[:, slot_index, :, None] * current)[..., None] * writes[
            :, slot_index, None, None, :
        ].astype(jnp.float32)
        state = decays[:, slot_index, :, None, None] * state + update
        value = jnp.einsum(
            "rhpn,rn->rhp",
            state,
            reads[:, slot_index].astype(jnp.float32),
            precision=lax.Precision.HIGHEST,
        )
        outputs.append(value + skip_gain[None, :, None] * current)
    return (state, jnp.stack(outputs, axis=1))


def on_device(
    stream_in,
    norm_gain,
    gate_weight,
    inner_weight,
    readwrite_weight,
    step_weight,
    conv_inner,
    conv_readwrite,
    decay_log,
    step_bias,
    skip_gain,
    gate_gain,
    out_weight,
    final_gain,
    embedding,
    state_cache,
    window_inner,
    window_readwrite,
    source_row,
    lengths,
    draft_ids,
):
    n_head = lax.axis_size("head")
    req_index = lax.axis_index("req")
    head_index = lax.axis_index("head")
    rows_dev = stream_in.shape[0]
    req_dev = lengths.shape[0]
    slots = rows_dev // req_dev
    all_req = source_row.shape[0]
    heads_dev = decay_log.shape[0]
    head_width = state_cache.shape[2]
    state_dim = state_cache.shape[3]
    inner_dev = inner_weight.shape[1]
    vocab_dev = embedding.shape[0]
    share = rows_dev // n_head
    first_req = req_index * req_dev
    takes_row = jnp.argsort(source_row)
    my_targets = lax.dynamic_slice_in_dim(takes_row, first_req, req_dev)
    send_order = jnp.argsort(my_targets)
    outgoing = (
        jnp.take(state_cache, send_order, axis=0),
        jnp.take(window_inner, send_order, axis=0),
        jnp.take(window_readwrite, send_order, axis=0),
    )
    arrived = (
        lax.all_to_all(outgoing[0], "req", split_axis=0, concat_axis=0, tiled=True),
        lax.all_to_all(outgoing[1], "req", split_axis=0, concat_axis=0, tiled=True),
        lax.all_to_all(outgoing[2], "req", split_axis=0, concat_axis=0, tiled=True),
    )
    my_sources = lax.dynamic_slice_in_dim(source_row, first_req, req_dev) // req_dev
    arrival_key = my_sources * all_req + first_req + jnp.arange(req_dev, dtype=jnp.int32)
    arrival_place = jnp.argsort(jnp.argsort(arrival_key))
    old_state = jnp.take(arrived[0], arrival_place, axis=0)
    old_inner = jnp.take(arrived[1], arrival_place, axis=0)
    old_readwrite = jnp.take(arrived[2], arrival_place, axis=0)
    stream = stream_in.astype(jnp.float32)
    normed = (stream / rms_of(stream) * norm_gain).astype(jnp.bfloat16)
    gate_val = jnp.dot(normed, gate_weight, preferred_element_type=jnp.float32).astype(jnp.bfloat16)
    inner_raw = jnp.dot(normed, inner_weight, preferred_element_type=jnp.float32).astype(
        jnp.bfloat16
    )
    readwrite_raw = jnp.dot(normed, readwrite_weight, preferred_element_type=jnp.float32).astype(
        jnp.bfloat16
    )
    step_raw = jnp.dot(normed, step_weight, preferred_element_type=jnp.float32).astype(jnp.bfloat16)
    full_inner = jnp.concatenate([old_inner, inner_raw.reshape(req_dev, slots, inner_dev)], axis=1)
    full_readwrite = jnp.concatenate(
        [old_readwrite, readwrite_raw.reshape(req_dev, slots, 2 * state_dim)], axis=1
    )
    inner_conv = conv_silu(full_inner, conv_inner)
    readwrite_conv = conv_silu(full_readwrite, conv_readwrite)
    taps = conv_inner.shape[0]
    tail_inner = last_rows(full_inner, lengths, taps - 1)
    tail_readwrite = last_rows(full_readwrite, lengths, taps - 1)
    live = (jnp.arange(slots, dtype=jnp.int32)[None, :] < lengths[:, None]).astype(jnp.float32)
    steps = (
        jax.nn.softplus(step_raw.astype(jnp.float32).reshape(req_dev, slots, heads_dev) + step_bias)
        * live[:, :, None]
    )
    decays = jnp.exp(-jnp.exp(decay_log) * steps)
    final_state, slot_out = run_slots(
        old_state.astype(jnp.float32),
        inner_conv.reshape(req_dev, slots, heads_dev, head_width),
        readwrite_conv[..., :state_dim],
        readwrite_conv[..., state_dim:],
        steps,
        decays,
        skip_gain,
    )
    state_after = final_state.astype(jnp.bfloat16)
    slot_values = slot_out.reshape(rows_dev, inner_dev)
    gated = slot_values * jax.nn.silu(gate_val.astype(jnp.float32))
    local_squares = jnp.sum(gated * gated, axis=1)
    total_squares = lax.psum(local_squares, "head")
    gated_normed = (
        gated / jnp.sqrt(total_squares[:, None] / (inner_dev * n_head) + epsilon) * gate_gain
    ).astype(jnp.bfloat16)
    live_tokens = live.reshape(rows_dev) > 0.5
    live_share = lax.dynamic_slice_in_dim(live_tokens, head_index * share, share)
    mixed = lax.psum(jnp.dot(gated_normed, out_weight, preferred_element_type=jnp.float32), "head")
    residual = stream + mixed
    scale = rms_of(residual)
    final_rows = (residual / scale * final_gain).astype(jnp.bfloat16)
    scale_share = lax.dynamic_slice_in_dim(scale[:, 0], head_index * share, share)
    hidden_rms = jnp.where(live_share, scale_share, 0.0)
    my_ids = lax.dynamic_slice_in_dim(draft_ids, req_index * rows_dev, rows_dev)
    start_rows = jnp.full((rows_dev,), lowest, jnp.float32)
    piece = lax.all_gather(embedding, "req", axis=0, tiled=True)
    logits = lax.dot_general(
        final_rows, piece, (((1,), (1,)), ((), ())), preferred_element_type=jnp.float32
    )
    spot = jnp.arange(piece.shape[0], dtype=jnp.int32)
    vocab_id = (spot // vocab_dev * n_head + head_index) * vocab_dev + spot % vocab_dev
    matched = jnp.where(my_ids[:, None] == vocab_id[None, :], logits, lowest)
    top_rows = jnp.maximum(start_rows, jnp.max(logits, axis=1))
    draft_rows = jnp.maximum(start_rows, jnp.max(matched, axis=1))
    top_rows, draft_rows = lax.pmax((top_rows, draft_rows), "head")
    top_share = lax.dynamic_slice_in_dim(top_rows, head_index * share, share)
    draft_share = lax.dynamic_slice_in_dim(draft_rows, head_index * share, share)
    top_logit = jnp.where(live_share, top_share, 0.0)
    draft_logit = jnp.where(live_share, draft_share, 0.0)
    return (state_after, tail_inner, tail_readwrite, hidden_rms, top_logit, draft_logit)


def solution(mesh):
    in_specs = (
        P("req", None),
        P(),
        P(None, "head"),
        P(None, "head"),
        P(),
        P(None, "head"),
        P(None, "head"),
        P(),
        P("head"),
        P("head"),
        P("head"),
        P("head"),
        P("head", None),
        P(),
        P(("req", "head"), None),
        P("req", "head", None, None),
        P("req", None, "head"),
        P("req", None, None),
        P(),
        P("req"),
        P(),
    )
    out_specs = (
        P("req", "head", None, None),
        P("req", None, "head"),
        P("req", None, None),
        P(("req", "head")),
        P(("req", "head")),
        P(("req", "head")),
    )
    return jax.shard_map(
        on_device, mesh=mesh, in_specs=in_specs, out_specs=out_specs, check_vma=False
    )
```

profile of v0, /device:TPU:0, one launch (start us, length us, event | category | flops | bytes accessed | tf_op | source)
XLA Modules:
  0.0 1580.2 jit_solution(14975383909090530984)
XLA Ops:
  8.0 3.3 sort.62
  11.4 1.2 sort.63
  12.7 1.4 gather_fusion.4
  14.8 7.3 all-to-all-start.2
  22.0 1.8 gather_fusion.2
  23.9 0.7 copy.55
  24.7 6.1 gather_fusion
  30.8 6.0 all-to-all-start.1
  36.8 5.5 broadcast_select_fusion.1
  42.3 2.0 all-to-all-done.1
  44.3 4.6 all-to-all-start
  50.2 4.2 convolution_convert_fusion.1
  54.5 1.2 sort.64
  55.8 1.2 sort.65
  58.2 0.7 gather_fusion.3
  59.9 103.2 %all-to-all-done = bf16[16,20,64,128]{3,2,1,0:T(8,128)(2,1)} async-done(((bf16[16,20,64,128]{3,2,1,0:T(8,128)(2,1)}), bf16[16,20,64,128]{3,2,1,0:T(8,128)(2,1)}, u32[]{:S(2)}, u32[]{:S(2)}) %all-to-all-start) | async-done | bytes 5242912 | tf_op jit(solution)/shard_map/all_to_all | solution.py:99
  163.1 6.1 gather_fusion.1
  169.1 14.9 fusion
  184.0 17.5 %fusion.1 = f32[16,1,20,64]{3,1,2,0:T(1,128)S(1)} fusion(f32[16,128]{1,0:T(8,128)S(1)} %get-tuple-element.47, f32[16,20,64]{2,1,0:T(8,128)S(1)} %get-tuple-element.40, f32[16,128]{1,0:T(8,128)S(1)} %get-tuple-element.48, f32[16,20,64]{2,1,0:T(8,128)S(1)} %get-tuple-element.37, f32[16,20]{1,0:T(8,128)S(1)} %bitcast.138, f32[16,20]{1,0:T(8,128)S(1)} %bitcast.142, ...), kind=kOutput, calls=%fused_computation.11 | convolution fusion | flops 52428800 | bytes 5511696 | tf_op jit(solution)/shard_map/rhpn,rn->rhp/dot_general | solution.py:43
  201.5 20.6 %fusion.16 = f32[16,1,20,64]{3,1,2,0:T(1,128)S(1)} fusion(f32[16,128]{1,0:T(8,128)S(1)} %get-tuple-element.46, f32[16,20,64]{2,1,0:T(8,128)S(1)} %get-tuple-element.39, f32[16,128]{1,0:T(8,128)S(1)} %get-tuple-element.47, f32[16,20,64]{2,1,0:T(8,128)S(1)} %get-tuple-element.40, f32[16,128]{1,0:T(8,128)S(1)} %get-tuple-element.48, ...), kind=kOutput, calls=%fused_computation.28 | convolution fusion | flops 60293120 | bytes 5603088 | tf_op jit(solution)/shard_map/rhpn,rn->rhp/dot_general | solution.py:43
  222.1 23.6 %fusion.2 = f32[16,1,20,64]{3,1,2,0:T(1,128)S(1)} fusion(f32[16,128]{1,0:T(8,128)S(1)} %get-tuple-element.45, f32[16,20,64]{2,1,0:T(8,128)S(1)} %get-tuple-element.38, f32[16,20]{1,0:T(8,128)S(1)} %bitcast.146, f32[16,128]{1,0:T(8,128)S(1)} %get-tuple-element.46, f32[16,20,64]{2,1,0:T(8,128)S(1)} %get-tuple-element.39, ...), kind=kOutput, calls=%fused_computation.12 | convolution fusion | flops 68157440 | bytes 5694480 | tf_op jit(solution)/shard_map/rhpn,rn->rhp/dot_general | solution.py:43
  246.2 4.3 multiply_reduce_fusion.1
  250.6 5.7 psum.14
  256.2 5.1 fusion.36
  262.0 0.8 dynamic_slice.26
  264.4 15.7 fusion.3
  280.1 14.6 all-reduce.3.cloned.1.call-done
  294.7 1.3 multiply_reduce_fusion
  296.0 1185.6 %all-gather.3.cloned.1.call-done = bf16[8,1572,2560]{2,1,0:T(8,128)(2,1)} async-done(((bf16[1,1572,2560]{2,1,0:T(8,128)(2,1)}), bf16[8,1572,2560]{2,1,0:T(8,128)(2,1)}) %all-gather.3.cloned.1.call-update) | async-done | bytes 64389136 | tf_op jit(solution)/shard_map/all_gather | solution.py:161
  1481.6 57.2 %reshape.415 = bf16[12576,2560]{1,0:T(8,128)(2,1)} reshape(bf16[8,1572,2560]{2,1,0:T(8,128)(2,1)} %all-gather.3.cloned.1.call-done) | data formatting | bytes 128778240
  1538.8 26.9 %select_reduce_fusion = (f32[64]{0:T(128)S(1)}, f32[64]{0:T(128)S(1)}) fusion(s32[12576]{0:T(1024)S(1)} %fusion.51, s32[64]{0:T(128)S(1)} %dynamic_slice.26, bf16[12576,2560]{1,0:T(8,128)(2,1)} %reshape.415, f32[64,2560]{1,0:T(8,128)S(1)} %copy-done.3, bf16[64,2560]{1,0:T(8,128)(2,1)S(1)} %copy-done.2, f32[2560]{0:T(1024)S(1)} %copy-done.4, ...), kind=kOutput, calls=%fused_computation.29 | convolution fusion | flops 4124942336 | bytes 65433728 | tf_op jit(solution)/shard_map/dot_general | solution.py:162
  1565.7 6.5 all-reduce
  (98 shorter events, 7.7 us)
Async XLA Ops:
  8.0 41.8 %copy-start = (bf16[2560,256]{1,0:T(8,128)(2,1)S(1)}, bf16[2560,256]{1,0:T(8,128)(2,1)}, u32[]{:S(2)}) copy-start(bf16[2560,256]{1,0:T(8,128)(2,1)} %param.31) | copy-start | bytes 3932164
  14.8 16.0 %all-to-all-start.2 = ((bf16[16,3,256]{2,1,0:T(4,128)(2,1)}), bf16[16,3,256]{2,1,0:T(4,128)(2,1)S(1)}, u32[]{:S(2)}, u32[]{:S(2)}) async-start(bf16[16,3,256]{2,1,0:T(4,128)(2,1)} %copy.59), calls=%async_computation.2 | async-start | bytes 65536 | tf_op jit(solution)/shard_map/all_to_all | solution.py:101
  30.8 13.6 all-to-all-start.1
  36.7 12.4 copy-start.2
  36.8 12.6 copy-start.12
  36.8 12.6 copy-start.13
  42.2 12.2 copy-start.10
  42.2 14.8 copy-start.5
  42.2 14.9 copy-start.14
  42.2 14.9 copy-start.7
  42.3 14.9 copy-start.8
  42.3 15.0 copy-start.9
  44.3 118.7 %all-to-all-start = ((bf16[16,20,64,128]{3,2,1,0:T(8,128)(2,1)}), bf16[16,20,64,128]{3,2,1,0:T(8,128)(2,1)}, u32[]{:S(2)}, u32[]{:S(2)}) async-start(bf16[16,20,64,128]{3,2,1,0:T(8,128)(2,1)} %broadcast_select_fusion.1), calls=%async_computation | async-start | bytes 10485760 | tf_op jit(solution)/shard_map/all_to_all | solution.py:99
  49.0 245.7 %all-reduce.3.cloned.1.call-start = ((), (), s32[]{:S(2)}) async-start(), calls=%async_computation.3 | async-start | bytes 1310720 | tf_op jit(solution)/shard_map/psum | solution.py:153
  169.1 14.9 slice-start
  169.1 14.9 slice-start.1
  222.1 23.6 %copy-start.11 = (f32[20]{0:T(128)S(1)}, f32[20]{0:T(128)}, u32[]{:S(2)}) copy-start(f32[20]{0:T(128)} %param.37) | copy-start | bytes 244
  245.7 10.5 copy-start.6
  261.3 1220.3 %all-gather.3.cloned.1.call-start = ((), (), s32[]{:S(2)}) async-start(), calls=%async_computation.4 | async-start | bytes 72622080 | tf_op jit(solution)/shard_map/all_gather | solution.py:161
  296.0 1242.8 %copy-start.3 = (f32[64,2560]{1,0:T(8,128)S(1)}, f32[64,2560]{1,0:T(8,128)}, u32[]{:S(2)}) copy-start(f32[64,2560]{1,0:T(8,128)} %all-reduce.3.cloned.1.call-done) | copy-start | bytes 1966084
  296.0 1242.8 %copy-start.4 = (f32[2560]{0:T(1024)S(1)}, f32[2560]{0:T(1024)}, u32[]{:S(2)}) copy-start(f32[2560]{0:T(1024)} %param.40) | copy-start | bytes 30724
  1538.8 34.0 %copy-start.1 = (bf16[2560,256]{1,0:T(8,128)(2,1)S(1)}, bf16[2560,256]{1,0:T(8,128)(2,1)}, u32[]{:S(2)}) copy-start(bf16[2560,256]{1,0:T(8,128)(2,1)} %param.31) | copy-start | bytes 3932164
Sparse Core Ops, SparseCore 0:
  261.4 33.2 all-reduce.2
Sparse Core Ops, SparseCore 1:
  263.3 1218.2 all-gather.2
where the time goes:
time: 1580 us
  waiting for transfers between devices  1310 us (83%)
  matrix products  118 us (7%)
  local copies, waits for them, and re-layouts  77 us (5%)
  other arithmetic  33.4 us (2%)
  starting transfers between devices  18.4 us (1%)
  between operations  16 us (1%)
    all_gather x1, waiting for transfers between devices, on_device(): piece = lax.all_gather(embedding, 'req', axis=0, tiled=True)  1190 us
    all_to_all x1, waiting for transfers between devices, on_device(): lax.all_to_all(outgoing[0], 'req', split_axis=0, concat_axis=0, tiled=True)  103 us
    dot_general x4, matrix products, run_slots(): jnp.einsum('rhpn,rn->rhp', state, reads[:, slot_index].astype(jnp.float32...  76.5 us
    unnamed x37, local copies, waits for them, and re-layouts  57.3 us
  transfers between devices with their start and end apart: 5, of which 4 were waited for; matrix products, arithmetic and copies ran while one was open for 3% of the time, Pallas kernels for 0%

commit v1 on v0

v1 whole, which is shorter than its diff:
```python
import functools

import jax
import jax.numpy as jnp
from jax import lax
from jax.experimental import pallas as pl
from jax.experimental.pallas import tpu as pltpu
from jax.sharding import PartitionSpec as P

epsilon = 1e-05
lowest = -1e30
f32 = jnp.float32
bf16 = jnp.bfloat16
i32 = jnp.int32
ANY = pl.BlockSpec(memory_space=pl.ANY)


def rms_of(values):
    return jnp.sqrt(jnp.mean(values * values, axis=-1, keepdims=True) + epsilon)


def send_body(req_dev, source, state, inner, readwrite, state_out, inner_out, readwrite_out, sems):
    me = lax.axis_index("req")
    arrays = ((state, state_out), (inner, inner_out), (readwrite, readwrite_out))

    def visit(request, slot):
        row = source[request]
        mine = lax.div(row, req_dev) == me

        @pl.when(mine)
        def _():
            for index, (held, sent) in enumerate(arrays):
                pltpu.make_async_copy(
                    held.at[lax.rem(row, req_dev)], sent.at[slot], sems.at[index, slot]
                ).start()

        return slot + mine.astype(i32)

    lax.fori_loop(0, source.shape[0], visit, jnp.int32(0))
    for slot in range(req_dev):
        for index, (held, sent) in enumerate(arrays):
            pltpu.make_async_copy(held.at[0], sent.at[slot], sems.at[index, slot]).wait()


def send_rows(source_row, state, inner, readwrite):
    req_dev = state.shape[0]
    return pl.pallas_call(
        functools.partial(send_body, req_dev),
        grid_spec=pltpu.PrefetchScalarGridSpec(
            num_scalar_prefetch=1,
            grid=(),
            in_specs=[ANY] * 3,
            out_specs=[ANY] * 3,
            scratch_shapes=[pltpu.SemaphoreType.DMA((3, req_dev))],
        ),
        out_shape=[jax.ShapeDtypeStruct(a.shape, a.dtype) for a in (state, inner, readwrite)],
        name="send_rows",
    )(source_row, state, inner, readwrite)


def read_body(home_row, state, reads, out):
    out[0] = lax.dot_general(
        reads[0], state[0], (((1,), (1,)), ((), ())), preferred_element_type=f32
    )


def read_states(home_row, state, reads):
    req_dev, slots, state_dim = reads.shape
    width = state.shape[1]
    return pl.pallas_call(
        read_body,
        grid_spec=pltpu.PrefetchScalarGridSpec(
            num_scalar_prefetch=1,
            grid=(req_dev,),
            in_specs=[
                pl.BlockSpec((1, width, state_dim), lambda k, rows: (rows[k], 0, 0)),
                pl.BlockSpec((1, slots, state_dim), lambda k, rows: (k, 0, 0)),
            ],
            out_specs=pl.BlockSpec((1, slots, width), lambda k, rows: (k, 0, 0)),
        ),
        out_shape=jax.ShapeDtypeStruct((req_dev, slots, width), f32),
        name="read_states",
    )(home_row, state, reads)


def update_body(heads, place, keep, state, weighted, writes, out):
    request = pl.program_id(0)
    added = lax.dot_general(
        weighted[0], writes[0], (((0,), (0,)), ((), ())), preferred_element_type=f32
    )
    width = added.shape[0] // heads
    for head in range(heads):
        rows = slice(head * width, (head + 1) * width)
        out[0, rows] = (
            state[0, rows].astype(f32) * keep[request, head] + added[rows]
        ).astype(bf16)


def update_states(place, keep, arrived, weighted, writes):
    req_dev, width, state_dim = arrived.shape
    terms = weighted.shape[1]
    return pl.pallas_call(
        functools.partial(update_body, keep.shape[1]),
        grid_spec=pltpu.PrefetchScalarGridSpec(
            num_scalar_prefetch=2,
            grid=(req_dev,),
            in_specs=[
                pl.BlockSpec((1, width, state_dim), lambda q, place, keep: (place[q], 0, 0)),
                pl.BlockSpec((1, terms, width), lambda q, place, keep: (q, 0, 0)),
                pl.BlockSpec((1, terms, state_dim), lambda q, place, keep: (q, 0, 0)),
            ],
            out_specs=pl.BlockSpec((1, width, state_dim), lambda q, place, keep: (q, 0, 0)),
        ),
        out_shape=jax.ShapeDtypeStruct(arrived.shape, bf16),
        name="update_states",
    )(place, keep, arrived, weighted, writes)


def conv_silu(window, weight):
    taps = weight.shape[0]
    count = window.shape[1] - taps + 1
    total = jnp.zeros((window.shape[0], count, window.shape[2]), f32)
    for tap in range(taps):
        total = total + window[:, tap : tap + count].astype(f32) * weight[tap].astype(f32)
    return jax.nn.silu(total).astype(bf16)


def last_rows(window, lengths, keep):
    places = jnp.arange(window.shape[1], dtype=i32)
    wide = window.astype(f32)
    picked = []
    for lag in range(keep):
        select = (places[None, :] == lengths[:, None] + lag).astype(f32)
        picked.append(jnp.sum(select[:, :, None] * wide, axis=1))
    return jnp.stack(picked, axis=1).astype(bf16)


def on_device(
    stream_in,
    norm_gain,
    gate_weight,
    inner_weight,
    readwrite_weight,
    step_weight,
    conv_inner,
    conv_readwrite,
    decay_log,
    step_bias,
    skip_gain,
    gate_gain,
    out_weight,
    final_gain,
    embedding,
    state_cache,
    window_inner,
    window_readwrite,
    source_row,
    lengths,
    draft_ids,
):
    n_req = lax.axis_size("req")
    n_head = lax.axis_size("head")
    req_index = lax.axis_index("req")
    head_index = lax.axis_index("head")
    rows_dev, model = stream_in.shape
    req_dev = lengths.shape[0]
    slots = rows_dev // req_dev
    all_req = source_row.shape[0]
    heads_dev, head_width, state_dim = state_cache.shape[1:]
    inner_dev = inner_weight.shape[1]
    vocab_dev = embedding.shape[0]
    share = rows_dev // n_head
    taps = conv_inner.shape[0]

    states = state_cache.reshape(req_dev, inner_dev, state_dim)
    leaving, leaving_inner, leaving_readwrite = send_rows(
        source_row, states, window_inner, window_readwrite
    )

    request = jnp.arange(all_req, dtype=i32)
    home = source_row // req_dev
    before = (home[None, :] == home[:, None]) & (request[None, :] < request[:, None])
    place = home * req_dev + jnp.sum(before.astype(i32), axis=1)
    at_home = place[None, :] == (req_index * req_dev + jnp.arange(req_dev, dtype=i32))[:, None]
    home_row = jnp.sum(jnp.where(at_home, (source_row % req_dev)[None, :], 0), axis=1)
    my_home = lax.dynamic_slice_in_dim(home, req_index * req_dev, req_dev)
    mine = jnp.arange(req_dev, dtype=i32)
    ahead = (my_home[None, :] < my_home[:, None]) | (
        (my_home[None, :] == my_home[:, None]) & (mine[None, :] < mine[:, None])
    )
    arrival = jnp.sum(ahead.astype(i32), axis=1)

    row = jnp.arange(rows_dev, dtype=i32)
    goes_to = jnp.repeat(arrival, slots) * slots + row % slots
    choose = (goes_to[None, :] == row[:, None]).astype(bf16)
    outgoing = jnp.dot(choose, stream_in, preferred_element_type=f32).astype(bf16)
    home_stream = lax.all_to_all(outgoing, "req", split_axis=0, concat_axis=0, tiled=True)
    got_inner = lax.all_to_all(leaving_inner, "req", split_axis=0, concat_axis=0, tiled=True)
    got_readwrite = lax.all_to_all(
        leaving_readwrite, "req", split_axis=0, concat_axis=0, tiled=True
    )
    arrived = lax.all_to_all(leaving, "req", split_axis=0, concat_axis=0, tiled=True)

    def project(stream):
        stream = stream.astype(f32)
        normed = (stream / rms_of(stream) * norm_gain).astype(bf16)
        inner = jnp.dot(normed, inner_weight, preferred_element_type=f32).astype(bf16)
        readwrite = jnp.dot(normed, readwrite_weight, preferred_element_type=f32).astype(bf16)
        step_raw = jnp.dot(normed, step_weight, preferred_element_type=f32).astype(bf16)
        return normed, inner, readwrite, step_raw

    def windows(inner, readwrite, old_inner, old_readwrite):
        full_inner = jnp.concatenate([old_inner, inner.reshape(req_dev, slots, inner_dev)], axis=1)
        full_readwrite = jnp.concatenate(
            [old_readwrite, readwrite.reshape(req_dev, slots, 2 * state_dim)], axis=1
        )
        return full_inner, full_readwrite

    def step_sizes(step_raw, live):
        raw = step_raw.astype(f32).reshape(req_dev, slots, heads_dev)
        steps = jax.nn.softplus(raw + step_bias) * live[:, :, None]
        return steps, jnp.exp(-jnp.exp(decay_log) * steps)

    spread = (
        jnp.arange(inner_dev, dtype=i32)[None, :] // head_width
        == jnp.arange(heads_dev, dtype=i32)[:, None]
    ).astype(f32)

    def expand(values):
        return jnp.dot(values, spread, precision=lax.Precision.HIGHEST)

    normed, inner, readwrite, step_raw = project(home_stream)
    gate = jnp.dot(normed, gate_weight, preferred_element_type=f32).astype(bf16)
    full_inner, full_readwrite = windows(inner, readwrite, leaving_inner, leaving_readwrite)
    conv_x = conv_silu(full_inner, conv_inner).astype(f32)
    conv_rw = conv_silu(full_readwrite, conv_readwrite)
    writes, reads = conv_rw[..., :state_dim], conv_rw[..., state_dim:]
    steps, decays = step_sizes(step_raw, jnp.ones((req_dev, slots), f32))
    from_state = read_states(home_row, states, reads)
    matches = jnp.einsum("rsn,rjn->rsj", reads, writes, preferred_element_type=f32)
    tables = []
    carried = None
    terms = []
    for slot in range(slots):
        decay = decays[:, slot]
        carried = decay if slot == 0 else carried * decay
        terms = [term * decay for term in terms] + [steps[:, slot]]
        tables.append(carried)
        for index, term in enumerate(terms):
            factor = term * matches[:, slot, index][:, None]
            if index == slot:
                factor = factor + skip_gain[None, :]
            tables.append(factor)
    wide = expand(jnp.concatenate(tables, axis=0)).reshape(len(tables), req_dev, inner_dev)
    outputs = []
    at = 0
    for slot in range(slots):
        value = wide[at] * from_state[:, slot]
        for index in range(slot + 1):
            value = value + wide[at + 1 + index] * conv_x[:, index]
        outputs.append(value)
        at += slot + 2
    slot_values = jnp.stack(outputs, axis=1).reshape(rows_dev, inner_dev)
    gated = slot_values * jax.nn.silu(gate.astype(f32))
    squares = jnp.sum(gated * gated, axis=1, keepdims=True)
    partial = jnp.dot(
        (gated * gate_gain).astype(bf16), out_weight, preferred_element_type=f32
    )
    packed = jnp.concatenate([partial, jnp.broadcast_to(squares, (rows_dev, 128))], axis=1)
    parts = lax.all_to_all(
        packed.reshape(n_head, share, model + 128), "head", split_axis=0, concat_axis=0, tiled=True
    )
    summed = jnp.sum(parts, axis=0)
    mixed = summed[:, :model] / jnp.sqrt(
        summed[:, model : model + 1] / (inner_dev * n_head) + epsilon
    )
    my_stream = lax.dynamic_slice_in_dim(home_stream, head_index * share, share).astype(f32)
    residual = my_stream + mixed
    scale = rms_of(residual)
    final = (residual / scale * final_gain).astype(bf16)

    tokens = n_req * rows_dev
    everyone = lax.all_gather(final, ("req", "head"), axis=0, tiled=True)
    ids = draft_ids.reshape(all_req, slots)
    chosen = place[None, :] == request[:, None]
    ids_at_home = jnp.sum(jnp.where(chosen[:, :, None], ids[None, :, :], 0), axis=1).reshape(tokens)
    logits = lax.dot_general(
        everyone, embedding, (((1,), (1,)), ((), ())), preferred_element_type=f32
    )
    first_id = (req_index * n_head + head_index) * vocab_dev
    vocab_id = first_id + jnp.arange(vocab_dev, dtype=i32)
    matched = jnp.where(ids_at_home[:, None] == vocab_id[None, :], logits, lowest)
    top = jnp.max(logits, axis=1)
    draft = jnp.max(matched, axis=1)
    first_row = req_index * rows_dev + head_index * share
    scales = lax.dynamic_update_slice_in_dim(
        jnp.full((tokens,), lowest, f32), scale[:, 0], first_row, axis=0
    )
    found = lax.pmax(jnp.stack([top, draft, scales]), ("req", "head"))
    my_req = share // slots
    first_req = req_index * req_dev + head_index * my_req
    my_place = lax.dynamic_slice_in_dim(place, first_req, my_req)
    pick = (my_place[:, None] == request[None, :])[None, :, :, None]
    by_request = found.reshape(3, 1, all_req, slots)
    own = jnp.max(jnp.where(pick, by_request, lowest), axis=2)
    my_lengths = lax.dynamic_slice_in_dim(lengths, head_index * my_req, my_req)
    live = jnp.arange(slots, dtype=i32)[None, :] < my_lengths[:, None]
    own = jnp.where(live[None], own, 0.0).reshape(3, share)

    _, inner_own, readwrite_own, step_own = project(stream_in)
    old_inner = jnp.take(got_inner, arrival, axis=0)
    old_readwrite = jnp.take(got_readwrite, arrival, axis=0)
    full_inner, full_readwrite = windows(inner_own, readwrite_own, old_inner, old_readwrite)
    tail_inner = last_rows(full_inner, lengths, taps - 1)
    tail_readwrite = last_rows(full_readwrite, lengths, taps - 1)
    conv_x = conv_silu(full_inner, conv_inner).astype(f32)
    writes = conv_silu(full_readwrite, conv_readwrite)[..., :state_dim]
    live = (jnp.arange(slots, dtype=i32)[None, :] < lengths[:, None]).astype(f32)
    steps, decays = step_sizes(step_own, live)
    keep = jnp.ones((req_dev, heads_dev), f32)
    terms = []
    for slot in reversed(range(slots)):
        terms.append(keep * steps[:, slot])
        keep = keep * decays[:, slot]
    terms = jnp.stack(terms[::-1], axis=1).reshape(rows_dev, heads_dev)
    weighted = expand(terms).reshape(req_dev, slots, inner_dev) * conv_x
    high = weighted.astype(bf16)
    low = (weighted - high.astype(f32)).astype(bf16)
    weighted = jnp.concatenate([high, low], axis=1)
    writes = jnp.concatenate([writes, writes], axis=1)

    arrived, weighted, writes, keep, own = lax.optimization_barrier(
        (arrived, weighted, writes, keep, own)
    )
    state_after = update_states(arrival, keep, arrived, weighted, writes).reshape(state_cache.shape)
    top_logit, draft_logit, hidden_rms = own
    return (state_after, tail_inner, tail_readwrite, hidden_rms, top_logit, draft_logit)


def solution(mesh):
    in_specs = (
        P("req", None),
        P(),
        P(None, "head"),
        P(None, "head"),
        P(),
        P(None, "head"),
        P(None, "head"),
        P(),
        P("head"),
        P("head"),
        P("head"),
        P("head"),
        P("head", None),
        P(),
        P(("req", "head"), None),
        P("req", "head", None, None),
        P("req", None, "head"),
        P("req", None, None),
        P(),
        P("req"),
        P(),
    )
    out_specs = (
        P("req", "head", None, None),
        P("req", None, "head"),
        P("req", None, None),
        P(("req", "head")),
        P(("req", "head")),
        P(("req", "head")),
    )
    return jax.shard_map(
        on_device, mesh=mesh, in_specs=in_specs, out_specs=out_specs, check_vma=False
    )
```

time: 1580 us -> 489 us (0.31)
  waiting for transfers between devices: 1310 us -> 144 us
  Pallas kernels: 0 us -> 192 us
  matrix products: 118 us -> 28.8 us
  local copies, waits for them, and re-layouts: 77 us -> 11.8 us
  blocking collectives: 12.1 us -> 54.7 us
    all_gather x1, waiting for transfers between devices: 1190 us -> 129 us  [on_device(): everyone = lax.all_gather(final, ('req', 'head'), axis=0, tiled=True)]
    pallas_call x0 -> x3, Pallas kernels: none -> 192 us  [the longest x1 167 us: send_rows(): pl.pallas_call(functools.partial(send_body, req_dev), grid_spec=pltpu.Pre...]
    all_to_all x3 -> x4, waiting for transfers between devices: 105 us -> 14.6 us  [the longest x1 7.64 us: on_device(): lax.all_to_all(outgoing, 'req', split_axis=0, concat_axis=0, tiled=True)]
    dot_general x10 -> x13, matrix products: 118 us -> 28.8 us  [the longest x1 8.63 us: on_device(): lax.dot_general(everyone, embedding, (((1,), (1,)), ((), ())), preferred_...]
    unnamed x37 -> x40, local copies, waits for them, and re-layouts: 57.3 us -> 3.51 us
    pmax x1, blocking collectives: 6.47 us -> 41.6 us  [on_device(): found = lax.pmax(jnp.stack([top, draft, scales]), ('req', 'head'))]
  transfers between devices with their start and end apart: 5 -> 5, of which waited for: 4 -> 3; matrix products, arithmetic and copies ran while one was open for 3% -> 6% of each run, Pallas kernels for 0% -> 0%
where the time goes in v1:
time: 489 us; the launch traced here: 487 us
  Pallas kernels  192 us (39%)
  waiting for transfers between devices  144 us (29%)
  blocking collectives  54.7 us (11%)
  matrix products  28.8 us (6%)
  starting transfers between devices  21.7 us (4%)
  other arithmetic  19.5 us (4%)
  between operations  14.6 us (3%)
  local copies, waits for them, and re-layouts  11.8 us (2%)
    pallas_call x1, Pallas kernels, send_rows(): pl.pallas_call(functools.partial(send_body, req_dev), grid_spec=pltpu.Pre...  167 us
    all_gather x1, waiting for transfers between devices, on_device(): everyone = lax.all_gather(final, ('req', 'head'), axis=0, tiled=True)  129 us
    pmax x1, blocking collectives, on_device(): found = lax.pmax(jnp.stack([top, draft, scales]), ('req', 'head'))  41.6 us
    pallas_call x1, Pallas kernels, update_states(): pl.pallas_call(functools.partial(update_body, keep.shape[1]), grid_spec=p...  13.6 us
    all_to_all x1, blocking collectives, on_device(): lax.all_to_all(packed.reshape(n_head, share, model + 128), 'head', split_...  13.2 us
    pallas_call x1, Pallas kernels, read_states(): pl.pallas_call(read_body, grid_spec=pltpu.PrefetchScalarGridSpec(num_scal...  11.6 us
  transfers between devices with their start and end apart: 5, of which 3 were waited for; matrix products, arithmetic and copies ran while one was open for 6% of the time, Pallas kernels for 0%

profile of v1, /device:TPU:0, one launch (start us, length us, event | category | flops | bytes accessed | tf_op | source)
XLA Modules:
  0.0 487.5 jit_solution(3259341961690707643)
XLA Ops:
  7.2 1.8 copy.82.inner
  9.0 1.4 copy.83.readwrite
  10.4 167.2 %send_rows.1 = (bf16[16,1280,128]{2,1,0:T(8,128)(2,1)}, bf16[16,3,1280]{2,1,0:T(4,128)(2,1)}, bf16[16,3,256]{2,1,0:T(4,128)(2,1)}) custom-call(s32[128]{0:T(128)} %source.1, bf16[16,1280,128]{2,1,0:T(8,128)(2,1)} %bitcast.149, bf16[16,3,1280]{2,1,0:T(4,128)(2,1)} %copy.82.inner, bf16[16,3,256]{2,1,0:T(4,128)(2,1)} %copy.83.readwrite), custom_call_target="tpu_custom_call" | custom-call | tf_op jit(solution)/shard_map/send_rows/pallas_call | solution.py:47
  177.6 7.2 %all-to-all-start.2 = ((bf16[16,3,256]{2,1,0:T(4,128)(2,1)}), bf16[16,3,256]{2,1,0:T(4,128)(2,1)S(1)}, u32[]{:S(2)}, u32[]{:S(2)}) async-start(bf16[16,3,256]{2,1,0:T(4,128)(2,1)} %get-tuple-element.16), calls=%async_computation.2 | async-start | bytes 65536 | tf_op jit(solution)/shard_map/all_to_all | solution.py:199
  186.0 0.9 fusion
  187.9 4.2 convolution_convert_fusion.3
  193.4 6.0 %all-to-all-start.1 = ((bf16[16,3,1280]{2,1,0:T(4,128)(2,1)}), bf16[16,3,1280]{2,1,0:T(4,128)(2,1)S(1)}, u32[]{:S(2)}, u32[]{:S(2)}) async-start(bf16[16,3,1280]{2,1,0:T(4,128)(2,1)} %get-tuple-element.15), calls=%async_computation.1 | async-start | bytes 327680 | tf_op jit(solution)/shard_map/all_to_all | solution.py:198
  200.0 6.9 %all-to-all-done.1 = bf16[16,3,1280]{2,1,0:T(4,128)(2,1)S(1)} async-done(((bf16[16,3,1280]{2,1,0:T(4,128)(2,1)}), bf16[16,3,1280]{2,1,0:T(4,128)(2,1)S(1)}, u32[]{:S(2)}, u32[]{:S(2)}) %all-to-all-start.1) | async-done | bytes 122912 | tf_op jit(solution)/shard_map/all_to_all | solution.py:198
  207.0 3.4 all-to-all-start.3
  211.4 7.6 %all-to-all-done.3 = bf16[8,8,2560]{2,1,0:T(8,128)(2,1)S(1)} async-done(((bf16[8,8,2560]{2,1,0:T(8,128)(2,1)}), bf16[8,8,2560]{2,1,0:T(8,128)(2,1)S(1)}, u32[]{:S(2)}, u32[]{:S(2)}) %all-to-all-start.3) | async-done | bytes 327712 | tf_op jit(solution)/shard_map/all_to_all | solution.py:197
  219.7 0.9 fusion.38
  221.7 4.2 convolution_convert_fusion.2
  228.7 0.8 fusion.92
  230.1 11.6 %read_states.1 = f32[16,4,1280]{2,1,0:T(4,128)} custom-call(s32[16]{0:T(128)} %select_reduce_fusion.3.home_row, bf16[16,1280,128]{2,1,0:T(8,128)(2,1)} %bitcast.150, bf16[16,4,128]{2,1,0:T(4,128)(2,1)} %slice.351.reads), custom_call_target="tpu_custom_call" | custom-call | tf_op jit(solution)/shard_map/read_states/pallas_call | solution.py:70
  242.0 2.6 fusion.12
  244.6 1.7 fusion.36
  246.3 1.6 fusion.35
  248.3 4.4 multiply_reduce_fusion.1
  252.7 4.1 fusion.13
  256.9 13.2 %all_to_all.32 = f32[4,16,2688]{2,1,0:T(8,128)S(1)} all-to-all(f32[4,16,2688]{2,1,0:T(8,128)S(1)} %bitcast.152), channel_id=1, replica_groups=mesh['req'=8,'head'=4] {'head'}, dimensions={0} | all-to-all | bytes 1376256 | tf_op jit(solution)/shard_map/all_to_all | solution.py:270
  270.1 4.8 all-to-all-start
  275.5 1.4 multiply_convert_fusion.3
  278.2 0.7 dynamic_slice.14
  279.0 0.7 dynamic_slice.13
  280.7 0.7 fusion.68
  282.3 0.8 fusion.7
  283.7 0.8 fusion.54
  285.4 0.9 pad_maximum_fusion.2.weighted
  286.4 129.4 %all-gather.2.cloned.1.call-done = bf16[512,2560]{1,0:T(8,128)(2,1)} async-done(((bf16[16,2560]{1,0:T(8,128)(2,1)}), bf16[512,2560]{1,0:T(8,128)(2,1)}) %all-gather.2.cloned.1.call-update) | async-done | bytes 2621456 | tf_op jit(solution)/shard_map/all_gather | solution.py:283
  415.8 8.6 %fusion.87 = (f32[512]{0:T(512)S(1)}, f32[512]{0:T(512)S(1)}) fusion(s32[1572]{0:T(1024)S(1)} %iota_add_fusion, s32[512]{0:T(512)S(1)} %eq.208, bf16[512,2560]{1,0:T(8,128)(2,1)} %all-gather.2.cloned.1.call-done, bf16[1572,2560]{1,0:T(8,128)(2,1)} %param.35), kind=kOutput, calls=%fused_computation.253 | convolution fusion | flops 4124122112 | bytes 10682512 | tf_op jit(solution)/shard_map/dot_general | solution.py:287
  424.7 41.6 %pmax.7 = f32[3,128,4]{2,1,0:T(8,128)S(1)} all-reduce(f32[3,128,4]{2,1,0:T(8,128)S(1)} %broadcast_in_dim.114), channel_id=1, replica_groups=mesh['req'=8,'head'=4] {'req','head'}, use_global_device_ids=true, to_apply=%region_11.12 | all-reduce | flops 1536 | bytes 12288 | tf_op jit(solution)/shard_map/pmax | solution.py:299
  467.1 13.6 %update_states.1 = bf16[16,1280,128]{2,1,0:T(8,128)(2,1)} custom-call(s32[16]{0:T(128)} %copy-done.14, f32[16,20]{1,0:T(8,128)} %get-tuple-element.17.keep, bf16[16,1280,128]{2,1,0:T(8,128)(2,1)} %all-to-all-done.state, bf16[16,8,1280]{2,1,0:T(8,128)(2,1)} %pad_maximum_fusion.2.weighted, bf16[16,8,128]{2,1,0:T(8,128)(2,1)} %pad_maximum_fusion.8.writes), custom_call_target="tpu_custom_call" | custom-call | tf_op jit(solution)/shard_map/update_states/pallas_call | solution.py:102
  (142 shorter events, 17.3 us)
Async XLA Ops:
  7.2 184.9 %copy-start = (bf16[2560,256]{1,0:T(8,128)(2,1)S(1)}, bf16[2560,256]{1,0:T(8,128)(2,1)}, u32[]{:S(2)}) copy-start(bf16[2560,256]{1,0:T(8,128)(2,1)} %param.25) | copy-start | bytes 3932164
  7.2 177.6 %copy-start.11 = (s32[128]{0:T(128)S(1)}, s32[128]{0:T(128)}, u32[]{:S(2)}) copy-start(s32[128]{0:T(128)} %source.1) | copy-start | bytes 1540
  7.2 178.6 %copy-start.1 = (bf16[64,2560]{1,0:T(8,128)(2,1)S(1)}, bf16[64,2560]{1,0:T(8,128)(2,1)}, u32[]{:S(2)}) copy-start(bf16[64,2560]{1,0:T(8,128)(2,1)} %param.21) | copy-start | bytes 983044
  7.2 179.7 %copy-start.9 = (s32[16]{0:T(128)S(1)}, s32[16]{0:T(128)}, u32[]{:S(2)}) copy-start(s32[16]{0:T(128)} %param.40) | copy-start | bytes 196
  7.2 179.7 %copy-start.5 = (bf16[4,1280]{1,0:T(4,128)(2,1)S(1)}, bf16[4,1280]{1,0:T(4,128)(2,1)}, u32[]{:S(2)}) copy-start(bf16[4,1280]{1,0:T(4,128)(2,1)} %param.27) | copy-start | bytes 30724
  7.2 180.4 %copy-start.16 = (bf16[2560,20]{0,1:T(8,128)(2,1)S(1)}, bf16[2560,20]{0,1:T(8,128)(2,1)}, u32[]{:S(2)}) copy-start(bf16[2560,20]{0,1:T(8,128)(2,1)} %param.26) | copy-start | bytes 307204
  7.2 180.4 %copy-start.17 = (f32[2560]{0:T(1024)S(1)}, f32[2560]{0:T(1024)}, u32[]{:S(2)}) copy-start(f32[2560]{0:T(1024)} %param.22) | copy-start | bytes 30724
  177.6 15.8 %all-to-all-start.2 = ((bf16[16,3,256]{2,1,0:T(4,128)(2,1)}), bf16[16,3,256]{2,1,0:T(4,128)(2,1)S(1)}, u32[]{:S(2)}, u32[]{:S(2)}) async-start(bf16[16,3,256]{2,1,0:T(4,128)(2,1)} %get-tuple-element.16), calls=%async_computation.2 | async-start | bytes 65536 | tf_op jit(solution)/shard_map/all_to_all | solution.py:199
  185.1 0.5 copy-start.14
  186.0 6.1 %copy-start.6 = (bf16[4,256]{1,0:T(4,128)(2,1)S(1)}, bf16[4,256]{1,0:T(4,128)(2,1)}, u32[]{:S(2)}) copy-start(bf16[4,256]{1,0:T(4,128)(2,1)} %param.28) | copy-start | bytes 6148
  187.9 11.6 %copy-start.18 = (f32[20]{0:T(128)S(1)}, f32[20]{0:T(128)}, u32[]{:S(2)}) copy-start(f32[20]{0:T(128)} %param.29) | copy-start | bytes 244
  192.1 27.6 %copy-start.4 = (bf16[16,3,256]{2,1,0:T(4,128)(2,1)S(1)}, bf16[16,3,256]{2,1,0:T(4,128)(2,1)}, u32[]{:S(2)}) copy-start(bf16[16,3,256]{2,1,0:T(4,128)(2,1)} %get-tuple-element.16) | copy-start | bytes 73732
  192.5 6.9 %copy-start.10 = (s32[128]{0:T(128)}, s32[128]{0:T(128)S(1)}, u32[]{:S(2)}) copy-start(s32[128]{0:T(128)S(1)} %multiply_add_fusion.5) | copy-start | bytes 1540
  193.4 13.6 %all-to-all-start.1 = ((bf16[16,3,1280]{2,1,0:T(4,128)(2,1)}), bf16[16,3,1280]{2,1,0:T(4,128)(2,1)S(1)}, u32[]{:S(2)}, u32[]{:S(2)}) async-start(bf16[16,3,1280]{2,1,0:T(4,128)(2,1)} %get-tuple-element.15), calls=%async_computation.1 | async-start | bytes 327680 | tf_op jit(solution)/shard_map/all_to_all | solution.py:198
  207.0 12.0 %all-to-all-start.3 = ((bf16[8,8,2560]{2,1,0:T(8,128)(2,1)}), bf16[8,8,2560]{2,1,0:T(8,128)(2,1)S(1)}, u32[]{:S(2)}, u32[]{:S(2)}) async-start(bf16[8,8,2560]{2,1,0:T(8,128)(2,1)} %fusion), calls=%async_computation.3 | async-start | bytes 655360 | tf_op jit(solution)/shard_map/all_to_all | solution.py:197
  210.5 15.4 %copy-start.2 = (bf16[16,3,256]{2,1,0:T(4,128)(2,1)}, bf16[16,3,256]{2,1,0:T(4,128)(2,1)S(1)}, u32[]{:S(2)}) copy-start(bf16[16,3,256]{2,1,0:T(4,128)(2,1)S(1)} %broadcast_select_fusion.1) | copy-start | bytes 73732
  219.3 6.6 %copy-start.15 = (f32[64]{0:T(128)}, f32[64]{0:T(128)S(1)}, u32[]{:S(2)}) copy-start(f32[64]{0:T(128)S(1)} %sqrt.43) | copy-start | bytes 772
  220.6 5.4 %copy-start.12 = (f32[20]{0:T(128)S(1)}, f32[20]{0:T(128)}, u32[]{:S(2)}) copy-start(f32[20]{0:T(128)} %param.30) | copy-start | bytes 244
  221.3 5.3 %copy-start.13 = (f32[20]{0:T(128)S(1)}, f32[20]{0:T(128)}, u32[]{:S(2)}) copy-start(f32[20]{0:T(128)} %param.31) | copy-start | bytes 244
  247.9 4.8 copy-start.7
  270.1 6.9 %copy-start.8 = (s32[512]{0:T(512)S(1)}, s32[512]{0:T(512)}, u32[]{:S(2)}) copy-start(s32[512]{0:T(512)} %param.41) | copy-start | bytes 6148
  270.1 11.4 %copy-start.3 = (bf16[16,3,256]{2,1,0:T(4,128)(2,1)S(1)}, bf16[16,3,256]{2,1,0:T(4,128)(2,1)}, u32[]{:S(2)}) copy-start(bf16[16,3,256]{2,1,0:T(4,128)(2,1)} %copy-done.2) | copy-start | bytes 73732
  270.1 196.5 %all-to-all-start = ((bf16[16,1280,128]{2,1,0:T(8,128)(2,1)}), bf16[16,1280,128]{2,1,0:T(8,128)(2,1)}, u32[]{:S(2)}, u32[]{:S(2)}) async-start(bf16[16,1280,128]{2,1,0:T(8,128)(2,1)} %get-tuple-element.14), calls=%async_computation | async-start | bytes 10485760 | tf_op jit(solution)/shard_map/all_to_all | solution.py:202
  274.9 141.0 %all-gather.2.cloned.1.call-start = ((), (), s32[]{:S(2)}) async-start(), calls=%async_computation.5 | async-start | bytes 2703360 | tf_op jit(solution)/shard_map/all_gather | solution.py:283
Sparse Core Ops, SparseCore 0:
  278.5 137.2 all-gather.1

commit v2 on v0

v2 whole, which is shorter than its diff:
```python
import functools

import jax
import jax.numpy as jnp
from jax import lax
from jax.experimental import pallas as pl
from jax.experimental.pallas import tpu as pltpu
from jax.sharding import PartitionSpec as P

epsilon = 1e-05
lowest = -1e30
f32 = jnp.float32
bf16 = jnp.bfloat16
i32 = jnp.int32
ANY = pl.BlockSpec(memory_space=pl.ANY)


def rms_of(values):
    return jnp.sqrt(jnp.mean(values * values, axis=-1, keepdims=True) + epsilon)


def pieces_body(where, size, rows, start, held, *refs):
    outs, (buffer, arrive, leave) = refs[:-3], refs[-3:]
    steps = [
        (distance, k, piece, order * size + k)
        for piece, distances in enumerate(where)
        for order, distance in enumerate(distances)
        for k in range(size)
    ]

    def read(index):
        distance, k = steps[index][:2]
        return pltpu.make_async_copy(
            held.at[rows[start[distance] + k]], buffer.at[index], arrive.at[index]
        )

    def write(index):
        piece, at = steps[index][2:]
        return pltpu.make_async_copy(buffer.at[index], outs[piece].at[at], leave.at[index])

    for index in range(len(steps)):
        read(index).start()
    for index in range(len(steps)):
        read(index).wait()
        write(index).start()
    for index in range(len(steps)):
        write(index).wait()


def take_pieces(rows, start, held, where, size):
    width, depth = held.shape[1:]
    count = size * sum(len(distances) for distances in where)
    return pl.pallas_call(
        functools.partial(pieces_body, tuple(where), size),
        grid_spec=pltpu.PrefetchScalarGridSpec(
            num_scalar_prefetch=2,
            grid=(),
            in_specs=[ANY],
            out_specs=[ANY] * len(where),
            scratch_shapes=[
                pltpu.VMEM((count, width, depth), held.dtype),
                pltpu.SemaphoreType.DMA((count,)),
                pltpu.SemaphoreType.DMA((count,)),
            ],
        ),
        out_shape=[
            jax.ShapeDtypeStruct((size * len(distances), width, depth), held.dtype)
            for distances in where
        ],
        cost_estimate=pl.CostEstimate(flops=1, bytes_accessed=1, transcendentals=0),
        name="take_pieces",
    )(rows, start, held)


def softplus(values):
    return jnp.maximum(values, 0.0) + jnp.log1p(jnp.exp(-jnp.abs(values)))


def silu(values):
    return values / (1.0 + jnp.exp(-values))


def home_body(
    sizes,
    order,
    tokens,
    norm_gain,
    old_inner,
    old_readwrite,
    conv_inner,
    conv_readwrite,
    heads,
    head_values,
    gate_gain,
    weights_inner,
    weights_readwrite,
    weights_step,
    weights_gate,
    weights_out,
    state,
    packed_out,
    partial_out,
    squares_out,
    stream_out,
    inner_held,
    readwrite_held,
    step_held,
    gate_held,
    out_held,
    state_held,
    normed,
    sums,
    sems,
    state_sems,
):
    requests, slots, state_dim, taps, chunks = sizes
    rows = requests * slots
    lag = taps - 1

    def parts(source, held, at):
        depth = source.shape[0] // chunks
        return [
            pltpu.make_async_copy(
                source.at[pl.ds(c * depth, depth)],
                held.at[pl.ds(c * depth, depth)],
                sems.at[at * chunks + c],
            )
            for c in range(chunks)
        ]

    inner_parts = parts(weights_inner, inner_held, 0)
    gate_parts = parts(weights_gate, gate_held, 1)
    out_parts = parts(weights_out, out_held, 2)
    small = [
        pltpu.make_async_copy(weights_readwrite, readwrite_held, sems.at[3 * chunks]),
        pltpu.make_async_copy(weights_step, step_held, sems.at[3 * chunks + 1]),
    ]
    states = [
        pltpu.make_async_copy(state.at[order[k]], state_held.at[k], state_sems.at[k])
        for k in range(requests)
    ]
    for copy in small + inner_parts + states + gate_parts + out_parts:
        copy.start()

    into = lax.broadcasted_iota(i32, (rows, rows), 0)
    origin = lax.broadcasted_iota(i32, (rows, rows), 1)
    by_slot = (origin == lax.rem(into, requests) * slots + lax.div(into, requests)).astype(bf16)
    stream_bf = jnp.dot(by_slot, tokens[...], preferred_element_type=f32)
    stream_out[...] = stream_bf.astype(bf16)
    scale = jnp.sqrt(jnp.mean(stream_bf * stream_bf, axis=1, keepdims=True) + epsilon)
    normed[...] = (stream_bf / scale * norm_gain[...]).astype(bf16)

    def project(held, copies):
        total = None
        depth = held.shape[0] // len(copies)
        for c, copy in enumerate(copies):
            copy.wait()
            span = pl.ds(c * depth, depth)
            part = jnp.dot(normed[:, span], held[span], preferred_element_type=f32)
            total = part if total is None else total + part
        return total.astype(bf16)

    readwrite = project(readwrite_held, small[:1])
    step_raw = project(step_held, small[1:])
    inner = project(inner_held, inner_parts)

    def of(values, slot):
        return values[slot * requests : (slot + 1) * requests]

    def convolve(old, new, weight):
        window = [old[j].astype(f32) for j in range(lag)]
        window = window + [of(new, slot).astype(f32) for slot in range(slots)]
        outs = []
        for slot in range(slots):
            total = None
            for tap in range(taps):
                part = window[slot + tap] * weight[tap : tap + 1].astype(f32)
                total = part if total is None else total + part
            outs.append(silu(total).astype(bf16))
        return outs

    x = convolve(old_inner, inner, conv_inner[...])
    vectors = convolve(old_readwrite, readwrite, conv_readwrite[...])
    writes = [v[:, :state_dim].astype(f32) for v in vectors]
    reads = [v[:, state_dim:].astype(f32) for v in vectors]

    bias, decay_rate, skip = (head_values[i : i + 1] for i in range(3))
    wide_step = jnp.dot(step_raw, heads[...], preferred_element_type=f32)
    steps = softplus(wide_step + bias)
    decays = jnp.exp(-decay_rate * steps)

    columns = jnp.concatenate(reads + [jnp.zeros((sums.shape[1] - rows, state_dim), f32)], axis=0).T
    column = lax.rem(lax.broadcasted_iota(i32, columns.shape, 1), requests)
    for k in range(requests):
        own = jnp.where(column == k, columns, 0.0).astype(bf16)
        states[k].wait()
        part = jnp.dot(state_held[k], own, preferred_element_type=f32)
        if k == 0:
            sums[...] = part
        else:
            sums[...] += part
    from_state = sums[...].T

    gate = project(gate_held, gate_parts)
    carried = None
    terms = []
    gated = []
    for slot in range(slots):
        decay, step = of(decays, slot), of(steps, slot)
        current = x[slot].astype(f32)
        carried = decay if carried is None else carried * decay
        terms = [term * decay for term in terms] + [step * current]
        value = carried * of(from_state, slot) + skip * current
        for j, term in enumerate(terms):
            match = jnp.sum(reads[slot] * writes[j], axis=1, keepdims=True)
            value = value + match * term
        gated.append(value * silu(of(gate, slot).astype(f32)))
    gated = jnp.concatenate(gated, axis=0)
    squares = jnp.sum(gated * gated, axis=1, keepdims=True)
    weighted = (gated * gate_gain[...]).astype(bf16)
    depth = weighted.shape[1] // chunks
    total = None
    for c, copy in enumerate(out_parts):
        copy.wait()
        part = jnp.dot(
            weighted[:, c * depth : (c + 1) * depth],
            out_held[pl.ds(c * depth, depth)],
            preferred_element_type=f32,
        )
        total = part if total is None else total + part
    partial_out[...] = total
    wide = jnp.broadcast_to(squares, (rows, 128))
    squares_out[...] = wide
    high = wide.astype(bf16)
    low = (wide - high.astype(f32)).astype(bf16)
    model = total.shape[1]
    packed_out[:, :model] = total.astype(bf16)
    packed_out[:, model : model + 128] = high
    packed_out[:, model + 128 :] = low


def home_tokens(order, tokens, small, big, state, slots, taps):
    rows, model = tokens.shape
    requests, width, state_dim = state.shape
    chunks = 5
    lanes = rows + -rows % 128
    in_vmem = pl.BlockSpec(memory_space=pltpu.VMEM)
    return pl.pallas_call(
        functools.partial(home_body, (requests, slots, state_dim, taps, chunks)),
        grid_spec=pltpu.PrefetchScalarGridSpec(
            num_scalar_prefetch=1,
            grid=(),
            in_specs=[in_vmem] * (1 + len(small)) + [ANY] * (len(big) + 1),
            out_specs=[in_vmem] * 4,
            scratch_shapes=[pltpu.VMEM(w.shape, w.dtype) for w in big]
            + [
                pltpu.VMEM(state.shape, state.dtype),
                pltpu.VMEM((rows, model), bf16),
                pltpu.VMEM((width, lanes), f32),
                pltpu.SemaphoreType.DMA((3 * chunks + 2,)),
                pltpu.SemaphoreType.DMA((requests,)),
            ],
        ),
        out_shape=[
            jax.ShapeDtypeStruct((rows, model + 256), bf16),
            jax.ShapeDtypeStruct((rows, model), f32),
            jax.ShapeDtypeStruct((rows, 128), f32),
            jax.ShapeDtypeStruct((rows, model), bf16),
        ],
        compiler_params=pltpu.CompilerParams(vmem_limit_bytes=48 << 20),
        cost_estimate=pl.CostEstimate(flops=1, bytes_accessed=1, transcendentals=0),
        name="home_tokens",
    )(order, tokens, *small, *big, state)


def update_body(where, size, heads, target, start, keep, weighted, writes, *refs):
    pieces = refs[: len(where)]
    out, before, after, arrive, leave = refs[-5:]
    count = len(where) * size

    def at(index):
        return start[where[index // size]] + index % size

    def read(index):
        return pltpu.make_async_copy(
            pieces[index // size].at[index % size], before.at[index], arrive.at[index]
        )

    def write(index):
        return pltpu.make_async_copy(after.at[index], out.at[target[at(index)]], leave.at[index])

    for index in range(count):
        read(index).start()
    width = weighted.shape[0] // heads
    for index in range(count):
        request = at(index)
        added = jnp.dot(weighted[...], writes[request], preferred_element_type=f32)
        read(index).wait()
        for head in range(heads):
            rows = slice(head * width, (head + 1) * width)
            after[index, rows] = (
                before[index, rows].astype(f32) * keep[request, head] + added[rows]
            ).astype(bf16)
        write(index).start()
    for index in range(count):
        write(index).wait()


def update_pieces(target, start, keep, weighted, writes, where, pieces, whole):
    size, width, state_dim = pieces[0].shape
    req_dev, heads = keep.shape
    count = len(where) * size
    return pl.pallas_call(
        functools.partial(update_body, tuple(where), size, heads),
        grid_spec=pltpu.PrefetchScalarGridSpec(
            num_scalar_prefetch=3,
            grid=(),
            in_specs=[pl.BlockSpec(memory_space=pltpu.VMEM)] * 2
            + [ANY] * (len(where) + len(whole)),
            out_specs=ANY,
            scratch_shapes=[
                pltpu.VMEM((count, width, state_dim), bf16),
                pltpu.VMEM((count, width, state_dim), bf16),
                pltpu.SemaphoreType.DMA((count,)),
                pltpu.SemaphoreType.DMA((count,)),
            ],
        ),
        out_shape=jax.ShapeDtypeStruct((req_dev, width, state_dim), bf16),
        input_output_aliases={5 + len(where): 0} if whole else {},
        compiler_params=pltpu.CompilerParams(vmem_limit_bytes=24 << 20),
        name="update_pieces",
    )(target, start, keep, weighted, writes, *pieces, *whole)


def head_body(vocab, first, ids, final, rows, top, draft):
    step = pl.program_id(0)
    depth = rows.shape[0]
    logits = lax.dot_general(
        rows[...], final[...], (((1,), (1,)), ((), ())), preferred_element_type=f32
    )
    row = step * depth + lax.broadcasted_iota(i32, logits.shape, 0)
    logits = jnp.where(row < vocab, logits, lowest)
    best = jnp.max(logits, axis=0, keepdims=True)
    match = jnp.max(
        jnp.where(row + first[0] == ids[...], logits, lowest), axis=0, keepdims=True
    )

    @pl.when(step == 0)
    def _():
        top[...] = best
        draft[...] = match

    @pl.when(step > 0)
    def _():
        top[...] = jnp.maximum(top[...], best)
        draft[...] = jnp.maximum(draft[...], match)


def head_logits(first, ids, final, embedding):
    vocab, model = embedding.shape
    tokens = final.shape[0]
    depth = 400
    return pl.pallas_call(
        functools.partial(head_body, vocab),
        grid_spec=pltpu.PrefetchScalarGridSpec(
            num_scalar_prefetch=1,
            grid=(pl.cdiv(vocab, depth),),
            in_specs=[
                pl.BlockSpec((1, tokens), lambda i, first: (0, 0)),
                pl.BlockSpec((tokens, model), lambda i, first: (0, 0)),
                pl.BlockSpec((depth, model), lambda i, first: (i, 0)),
            ],
            out_specs=[pl.BlockSpec((1, tokens), lambda i, first: (0, 0))] * 2,
        ),
        out_shape=[jax.ShapeDtypeStruct((1, tokens), f32)] * 2,
        compiler_params=pltpu.CompilerParams(vmem_limit_bytes=24 << 20),
        cost_estimate=pl.CostEstimate(
            flops=2 * vocab * model * tokens,
            bytes_accessed=2 * vocab * model,
            transcendentals=0,
        ),
        name="head_logits",
    )(first, ids, final, embedding)


def on_device(
    stream_in,
    norm_gain,
    gate_weight,
    inner_weight,
    readwrite_weight,
    step_weight,
    conv_inner,
    conv_readwrite,
    decay_log,
    step_bias,
    skip_gain,
    gate_gain,
    out_weight,
    final_gain,
    embedding,
    state_cache,
    window_inner,
    window_readwrite,
    source_row,
    lengths,
    draft_ids,
):
    n_req = lax.axis_size("req")
    n_head = lax.axis_size("head")
    req_index = lax.axis_index("req")
    head_index = lax.axis_index("head")
    rows_dev, model = stream_in.shape
    req_dev = lengths.shape[0]
    slots = rows_dev // req_dev
    all_req = source_row.shape[0]
    heads_dev, head_width, state_dim = state_cache.shape[1:]
    inner_dev = inner_weight.shape[1]
    vocab_dev = embedding.shape[0]
    share = rows_dev // n_head
    taps = conv_inner.shape[0]

    each = req_dev // n_req
    states = state_cache.reshape(req_dev, inner_dev, state_dim)

    def swap(values, axis, mask):
        return lax.ppermute(values, axis, [(i, i ^ mask) for i in range(lax.axis_size(axis))])

    request = jnp.arange(all_req, dtype=i32)
    block = request // req_dev
    home = source_row // req_dev
    before = (
        (home[None, :] == home[:, None])
        & (block[None, :] == block[:, None])
        & (request[None, :] < request[:, None])
    )
    rank = jnp.sum(before.astype(i32), axis=1)
    place = (block ^ home) * each + rank
    listed = jnp.arange(req_dev, dtype=i32)[:, None]
    is_home = (listed == place[None, :]) & (home == req_index)[None, :]
    is_target = (listed == place[None, :]) & (block == req_index)[None, :]
    start = jnp.arange(n_req, dtype=i32) * each
    home_row = jnp.sum(jnp.where(is_home, (source_row % req_dev)[None, :], 0), axis=1)
    target = jnp.sum(jnp.where(is_target, (request % req_dev)[None, :], 0), axis=1)

    mine = jnp.arange(req_dev, dtype=i32)
    to_target = (target[:, None] == mine[None, :]).astype(bf16)
    to_home = (home_row[:, None] == mine[None, :]).astype(bf16)
    row = jnp.arange(rows_dev, dtype=i32)
    source_token = jnp.repeat(target, slots) * slots + row % slots
    tokens_out = jnp.dot(
        (source_token[:, None] == row[None, :]).astype(bf16),
        stream_in,
        preferred_element_type=f32,
    ).astype(bf16)

    def choose(selector, values):
        return jnp.einsum("kr,rjc->jkc", selector, values, preferred_element_type=f32).astype(bf16)

    home_inner = choose(to_home, window_inner)
    home_readwrite = choose(to_home, window_readwrite)
    lag = taps - 1
    packed_inner = home_inner.reshape(lag, n_req, each * inner_dev).transpose(1, 0, 2)
    packed_readwrite = (
        home_readwrite.reshape(lag, n_req, each * 2 * state_dim)
        .transpose(1, 0, 2)
        .reshape(n_req, 1, lag * each * 2 * state_dim)
    )
    letters = jnp.concatenate(
        [
            tokens_out.reshape(n_req, each * slots, model),
            jnp.pad(packed_inner, ((0, 0), (0, 0), (0, model - packed_inner.shape[2]))),
            jnp.pad(packed_readwrite, ((0, 0), (0, 0), (0, model - packed_readwrite.shape[2]))),
        ],
        axis=1,
    )
    outgoing = letters
    pairs = [letters[:2]]
    for mask in range(2, n_req, 2):
        pairs.append(swap(letters[mask : mask + 2], "req", mask))
    direct = [d for d in range(1, n_req) if d > 3] if n_req > 3 else []
    phases = ([n_req - 2], [d for d in direct if d != n_req - 2])
    home_row_a, outgoing = lax.optimization_barrier((home_row, outgoing))
    pair, *leaving_a = take_pieces(
        home_row_a, start, states, [(2, 3)] + [(d,) for d in phases[0]], each
    )
    pairs, pair, leaving_a = lax.optimization_barrier((pairs, pair, leaving_a))
    arrived = {}
    for d, value in zip(phases[0], leaving_a):
        arrived[d] = swap(value, "req", d)
    pair = swap(pair, "req", 2)
    arrived[2] = pair[:each]
    kept = jnp.stack([both[0] for both in pairs])
    passed = swap(jnp.stack([both[1] for both in pairs]), "req", 1)
    letters = jnp.stack([kept, passed], axis=1).reshape(letters.shape)

    home_stream = letters[:, : each * slots].reshape(rows_dev, model)
    got_inner = (
        letters[:, each * slots : each * slots + lag, : each * inner_dev]
        .transpose(1, 0, 2)
        .reshape(lag, req_dev, inner_dev)
    )
    got_readwrite = (
        letters[:, each * slots + lag, : lag * each * 2 * state_dim]
        .reshape(n_req, lag, each * 2 * state_dim)
        .transpose(1, 0, 2)
        .reshape(lag, req_dev, 2 * state_dim)
    )

    def project(stream):
        stream = stream.astype(f32)
        normed = (stream / rms_of(stream) * norm_gain).astype(bf16)
        inner = jnp.dot(normed, inner_weight, preferred_element_type=f32).astype(bf16)
        readwrite = jnp.dot(normed, readwrite_weight, preferred_element_type=f32).astype(bf16)
        step_raw = jnp.dot(normed, step_weight, preferred_element_type=f32).astype(bf16)
        return normed, inner, readwrite, step_raw

    def windows(old, new):
        new = new.reshape(req_dev, slots, new.shape[1])
        return [old[j] for j in range(lag)] + [new[:, s] for s in range(slots)]

    def conv_silu(rows, weight):
        outs = []
        for slot in range(slots):
            total = jnp.zeros(rows[0].shape, f32)
            for tap in range(taps):
                total = total + rows[slot + tap].astype(f32) * weight[tap].astype(f32)
            outs.append(jax.nn.silu(total).astype(bf16))
        return outs

    def step_sizes(step_raw, live):
        raw = step_raw.astype(f32).reshape(req_dev, slots, heads_dev)
        steps = jax.nn.softplus(raw + step_bias) * live[:, :, None]
        return steps, jnp.exp(-jnp.exp(decay_log) * steps)

    spread = (
        jnp.arange(inner_dev, dtype=i32)[None, :] // head_width
        == jnp.arange(heads_dev, dtype=i32)[:, None]
    ).astype(f32)

    def expand(values):
        return jnp.dot(values, spread, precision=lax.Precision.HIGHEST)

    head_values = jnp.repeat(
        jnp.stack([step_bias, jnp.exp(decay_log), skip_gain]), head_width, axis=1
    )
    packed, partial, squares, home_stream = home_tokens(
        home_row,
        home_stream,
        (
            norm_gain[None, :],
            home_inner,
            home_readwrite,
            conv_inner,
            conv_readwrite,
            spread.astype(bf16),
            head_values,
            gate_gain[None, :],
        ),
        (inner_weight, readwrite_weight, step_weight, gate_weight, out_weight),
        states,
        slots,
        taps,
    )

    def rows_of(values, index):
        return lax.dynamic_slice_in_dim(values, index * share, share)

    mixed = rows_of(partial, head_index)
    total = rows_of(squares, head_index)[:, :1]
    for mask in range(1, n_head):
        part = swap(rows_of(packed, head_index ^ mask), "head", mask).astype(f32)
        mixed = mixed + part[:, :model]
        total = total + part[:, model : model + 1] + part[:, model + 128 : model + 129]
    mixed = mixed / jnp.sqrt(total / (inner_dev * n_head) + epsilon)
    residual = rows_of(home_stream, head_index).astype(f32) + mixed
    scale = rms_of(residual)
    final = (residual / scale * final_gain).astype(bf16)

    distance = [0]
    final, home_row_b = lax.optimization_barrier((final, home_row))
    local, neighbour, *leaving_b = take_pieces(
        home_row_b, start, states, [(0,), (1,)] + [(d,) for d in phases[1]], each
    )
    arrived[0] = local
    for d, value in zip(phases[1], leaving_b):
        arrived[d] = swap(value, "req", d)
    everyone = final
    for step, (axis, masks) in enumerate((
        ("req", range(2, n_req, 2)),
        ("req", (1,)),
        ("head", range(2, n_head, 2)),
        ("head", (1,)),
    )):
        if step == 3:
            first_late = phases[1][0]
            everyone, arrived[first_late] = lax.optimization_barrier(
                (everyone, arrived[first_late])
            )
        everyone = jnp.concatenate([everyone] + [swap(everyone, axis, m) for m in masks], axis=0)
        if step == 1:
            passed_on = jnp.concatenate([neighbour, pair[each:]])
            everyone, passed_on = lax.optimization_barrier((everyone, passed_on))
            passed_on = swap(passed_on, "req", 1)
            arrived[1], arrived[3] = passed_on[:each], passed_on[each:]
        unit = n_head if axis == "req" else 1
        distance = distance + [e ^ (m * unit) for m in masks for e in distance]

    tokens = n_req * rows_dev
    my_req = share // slots
    my_device = req_index * n_head + head_index
    local = jnp.arange(slots, dtype=i32)[None, :] * req_dev + place[:, None]
    local = local.reshape(tokens)
    from_device = jnp.repeat(home, slots) * n_head + local // share
    away = (from_device ^ my_device)[:, None] == jnp.array(distance, dtype=i32)[None, :]
    found_at = jnp.sum(
        jnp.where(away, jnp.arange(len(distance), dtype=i32)[None, :], 0), axis=1
    ) * share + local % share
    token = jnp.arange(tokens, dtype=i32)
    pick = found_at[:, None] == token[None, :]
    ids_here = jnp.sum(jnp.where(pick, draft_ids[:, None], 0), axis=0)
    first_row = jnp.full((1,), my_device * vocab_dev, i32)
    top, draft = head_logits(first_row, ids_here[None, :], everyone, embedding)
    held = [1, 3] + phases[1][1:2]
    top, draft, *values = lax.optimization_barrier((top, draft, *(arrived[d] for d in held)))
    arrived.update(zip(held, values))
    scales = jnp.concatenate([scale[:, 0], jnp.full((tokens - share,), lowest, f32)])
    found = jnp.concatenate([top, draft, scales[None, :]])
    found = jnp.max(jnp.where(pick[None], found[:, None, :], lowest), axis=2)
    found = found.reshape(3, n_req, n_head, share)

    def for_head(index):
        return lax.dynamic_index_in_dim(found, index, axis=2, keepdims=False)

    best = for_head(head_index)
    for mask in range(1, n_head):
        best = jnp.maximum(best, swap(for_head(head_index ^ mask), "head", mask))


    def for_req(distance):
        return lax.dynamic_index_in_dim(best, req_index ^ distance, axis=1, keepdims=False)

    far = swap(jnp.stack([for_req(mask ^ 1) for mask in range(0, n_req, 2)]), "req", 1)
    own = jnp.maximum(for_req(0), far[0])
    for mask in range(2, n_req, 2):
        own = jnp.maximum(own, swap(jnp.maximum(for_req(mask), far[mask // 2]), "req", mask))
    my_lengths = lax.dynamic_slice_in_dim(lengths, head_index * my_req, my_req)
    live = jnp.arange(slots, dtype=i32)[None, :] < my_lengths[:, None]
    own = jnp.where(live.reshape(1, share), own, 0.0)

    tokens_out, got_inner, got_readwrite, _ = lax.optimization_barrier(
        (tokens_out, got_inner, got_readwrite, final)
    )
    _, inner, readwrite, step_raw = project(tokens_out)
    rows_inner = windows(got_inner, inner)
    rows_readwrite = windows(got_readwrite, readwrite)
    my_lengths = jnp.sum(jnp.where(to_target > 0, lengths[None, :], 0), axis=1)

    def tails(rows):
        picked = []
        for j in range(lag):
            value = rows[j + 1]
            for length in range(2, slots + 1):
                value = jnp.where(my_lengths[:, None] == length, rows[j + length], value)
            picked.append(value)
        picked = jnp.stack(picked, axis=1)
        return jnp.einsum("kr,kjc->rjc", to_target, picked, preferred_element_type=f32).astype(bf16)

    tail_inner = tails(rows_inner)
    tail_readwrite = tails(rows_readwrite)
    conv_x = conv_silu(rows_inner, conv_inner)
    writes = jnp.stack(conv_silu(rows_readwrite, conv_readwrite), axis=1)[..., :state_dim]
    live = (jnp.arange(slots, dtype=i32)[None, :] < my_lengths[:, None]).astype(f32)
    steps, decays = step_sizes(step_raw, live)
    keep = jnp.ones((req_dev, heads_dev), f32)
    terms = []
    for slot in reversed(range(slots)):
        terms.append(keep * steps[:, slot])
        keep = keep * decays[:, slot]
    wide = expand(jnp.concatenate(terms[::-1], axis=0)).reshape(slots, req_dev, inner_dev)
    weighted = jnp.stack([wide[s] * conv_x[s].astype(f32) for s in range(slots)], axis=1)
    high = weighted.astype(bf16)
    low = (weighted - high.astype(f32)).astype(bf16)
    count = 2 * slots * req_dev
    weighted = jnp.concatenate([high, low], axis=1).reshape(count, inner_dev).T
    writes = jnp.concatenate([writes, writes], axis=1).reshape(1, count, state_dim)
    owner = jnp.arange(count, dtype=i32)[None, :, None] // (2 * slots)
    writes = jnp.where(owner == mine[:, None, None], writes, 0)

    update = functools.partial(update_pieces, target, start, keep, weighted, writes)
    early = [0, 1, 2, 3] + phases[0] + phases[1][:2]
    after = update(early, [arrived[d] for d in early], ())
    late = phases[1][2:]
    after = update(late, [arrived[d] for d in late], (after,))
    state_after = after.reshape(state_cache.shape)
    top_logit, draft_logit, hidden_rms = own
    return (state_after, tail_inner, tail_readwrite, hidden_rms, top_logit, draft_logit)


def solution(mesh):
    in_specs = (
        P("req", None),
        P(),
        P(None, "head"),
        P(None, "head"),
        P(),
        P(None, "head"),
        P(None, "head"),
        P(),
        P("head"),
        P("head"),
        P("head"),
        P("head"),
        P("head", None),
        P(),
        P(("req", "head"), None),
        P("req", "head", None, None),
        P("req", None, "head"),
        P("req", None, None),
        P(),
        P("req"),
        P(),
    )
    out_specs = (
        P("req", "head", None, None),
        P("req", None, "head"),
        P("req", None, None),
        P(("req", "head")),
        P(("req", "head")),
        P(("req", "head")),
    )
    return jax.shard_map(
        on_device, mesh=mesh, in_specs=in_specs, out_specs=out_specs, check_vma=False
    )
```

time: 1580 us -> 195 us (0.12)
  waiting for transfers between devices: 1310 us -> 90.3 us
  matrix products: 118 us -> 9.19 us
  local copies, waits for them, and re-layouts: 77 us -> 14 us
  Pallas kernels: 0 us -> 35.9 us
  other arithmetic: 33.4 us -> 11.6 us
    all_gather x1 -> x0, waiting for transfers between devices: 1190 us -> none  [on_device(): piece = lax.all_gather(embedding, 'req', axis=0, tiled=True)]
    dot_general x10 -> x9, matrix products: 118 us -> 9.19 us  [the longest x1 4.19 us: project(): jnp.dot(normed, inner_weight, preferred_element_type=f32).astype(bf16)]
    all_to_all x3 -> x0, waiting for transfers between devices: 105 us -> none  [the longest x1 103 us: on_device(): lax.all_to_all(outgoing[0], 'req', split_axis=0, concat_axis=0, tiled=True)]
    ppermute x0 -> x26, waiting for transfers between devices: none -> 90.3 us  [swap(): lax.ppermute(values, axis, [(i, i ^ mask) for i in range(lax.axis_size(ax...]
    unnamed x37 -> x105, local copies, waits for them, and re-layouts: 57.3 us -> 6.32 us
    pallas_call x0 -> x6, Pallas kernels: none -> 35.9 us  [the longest x1 13.5 us: home_tokens(): pl.pallas_call(functools.partial(home_body, (requests, slots, state_dim,...]
    ppermute x0 -> x26, starting transfers between devices: none -> 31.3 us  [swap(): lax.ppermute(values, axis, [(i, i ^ mask) for i in range(lax.axis_size(ax...]
    all_to_all x3 -> x0, starting transfers between devices: 17.9 us -> none  [the longest x1 7.28 us: on_device(): lax.all_to_all(outgoing[2], 'req', split_axis=0, concat_axis=0, tiled=True)]
  transfers between devices with their start and end apart: 5 -> 26, of which waited for: 4 -> 10; matrix products, arithmetic and copies ran while one was open for 3% -> 12% of each run, Pallas kernels for 0% -> 18%
where the time goes in v2:
time: 195 us; the launch traced here: 194 us
  waiting for transfers between devices  90.3 us (46%)
  Pallas kernels  35.9 us (18%)
  starting transfers between devices  31.3 us (16%)
  local copies, waits for them, and re-layouts  14 us (7%)
  other arithmetic  11.6 us (6%)
  matrix products  9.19 us (5%)
  between operations  2.01 us (1%)
    ppermute x26, waiting for transfers between devices, swap(): lax.ppermute(values, axis, [(i, i ^ mask) for i in range(lax.axis_size(ax...  90.3 us
    ppermute x26, starting transfers between devices, swap(): lax.ppermute(values, axis, [(i, i ^ mask) for i in range(lax.axis_size(ax...  31.3 us
    pallas_call x1, Pallas kernels, home_tokens(): pl.pallas_call(functools.partial(home_body, (requests, slots, state_dim,...  13.5 us
    pallas_call x2, Pallas kernels, update_pieces(): pl.pallas_call(functools.partial(update_body, tuple(where), size, heads),...  10.2 us
    pallas_call x2, Pallas kernels, take_pieces(): pl.pallas_call(functools.partial(pieces_body, tuple(where), size), grid_s...  6.71 us
    unnamed x105, local copies, waits for them, and re-layouts  6.32 us
    pallas_call x1, Pallas kernels, head_logits(): pl.pallas_call(functools.partial(head_body, vocab), grid_spec=pltpu.Prefe...  5.49 us
    dot_general x1, matrix products, project(): jnp.dot(normed, inner_weight, preferred_element_type=f32).astype(bf16)  4.19 us
  transfers between devices with their start and end apart: 26, of which 10 were waited for; matrix products, arithmetic and copies ran while one was open for 12% of the time, Pallas kernels for 18%

profile of v2, /device:TPU:0, one launch (start us, length us, event | category | flops | bytes accessed | tf_op | source)
XLA Modules:
  0.0 194.3 jit_solution(15513665550803538851)
XLA Ops:
  2.9 1.1 fusion.old_inner
  5.2 5.0 %collective-permute-start.2 = (bf16[2,12,2560]{2,1,0:T(8,128)(2,1)S(1)}, bf16[2,12,2560]{2,1,0:T(8,128)(2,1)S(1)}, u32[]{:S(2)}, u32[]{:S(2)}) collective-permute-start(bf16[2,12,2560]{2,1,0:T(8,128)(2,1)S(1)} %get-tuple-element.100), channel_id=1, source_target_pairs={{0,24},{4,28},{8,16},{12,20},{16,8},{20,12},{24,0},{28,4},{1,25},{... | collective-permute-start | bytes 368648 | tf_op jit(solution)/shard_map/ppermute | solution.py:427
  16.1 3.2 %take_pieces.2 = (bf16[4,1280,128]{2,1,0:T(8,128)(2,1)}, bf16[2,1280,128]{2,1,0:T(8,128)(2,1)}) custom-call(s32[16]{0:T(128)} %copy-done.10, s32[8]{0:T(128)} %iota_multiply_fusion.1.start, bf16[16,1280,128]{2,1,0:T(8,128)(2,1)} %bitcast.173), custom_call_target="tpu_custom_call" | custom-call | flops 1 | bytes 1 | tf_op jit(solution)/shard_map/take_pieces/pallas_call | solution.py:53
  21.3 2.8 %collective-permute-done.1 = bf16[2,12,2560]{2,1,0:T(8,128)(2,1)S(1)} collective-permute-done((bf16[2,12,2560]{2,1,0:T(8,128)(2,1)S(1)}, bf16[2,12,2560]{2,1,0:T(8,128)(2,1)S(1)}, u32[]{:S(2)}, u32[]{:S(2)}) %collective-permute-start.1) | collective-permute-done | bytes 122912 | tf_op jit(solution)/shard_map/ppermute | solution.py:427
  24.3 1.6 collective-permute-start.3
  25.9 2.5 %collective-permute-start.18 = (bf16[2,1280,128]{2,1,0:T(8,128)(2,1)}, bf16[2,1280,128]{2,1,0:T(8,128)(2,1)}, u32[]{:S(2)}, u32[]{:S(2)}) collective-permute-start(bf16[2,1280,128]{2,1,0:T(8,128)(2,1)} %get-tuple-element.69), channel_id=1, source_target_pairs={{0,24},{4,28},{8,16},{12,20},{16,8},{20,12},{24,0},{28,4},{1,25},{... | collective-permute-start | bytes 1966088 | tf_op jit(solution)/shard_map/ppermute | solution.py:427
  28.4 4.7 %collective-permute-done.3 = bf16[4,12,2560]{2,1,0:T(8,128)(2,1)S(1)} collective-permute-done((bf16[4,12,2560]{2,1,0:T(8,128)(2,1)S(1)}, bf16[4,12,2560]{2,1,0:T(8,128)(2,1)S(1)}, u32[]{:S(2)}, u32[]{:S(2)}) %collective-permute-start.3) | collective-permute-done | bytes 245792 | tf_op jit(solution)/shard_map/ppermute | solution.py:427
  35.2 13.5 %home_tokens.1 = (bf16[64,2816]{1,0:T(8,128)(2,1)S(1)}, f32[64,2560]{1,0:T(8,128)S(1)}, f32[64,128]{1,0:T(8,128)S(1)}, bf16[64,2560]{1,0:T(8,128)(2,1)S(1)}) custom-call(s32[16]{0:T(128)S(1)} %copy-done.11, bf16[64,2560]{1,0:T(8,128)(2,1)S(1)} %bitcast.169, f32[1,2560]{1,0:T(1,128)S(1)} %broadcast_in_dim.304.norm_gain, ...), custom_call_target="tpu_custom_call" | custom-call | flops 1 | bytes 1 | tf_op jit(solution)/shard_map/home_tokens/pallas_call | solution.py:248
  48.9 1.6 collective-permute-start.6
  57.3 4.2 %convolution_convert_fusion.1 = bf16[64,1280]{1,0:T(8,128)(2,1)S(1)} fusion(bf16[2560,1280]{1,0:T(8,128)(2,1)} %weights_inner.1, bf16[64,2560]{1,0:T(8,128)(2,1)S(1)} %copy-done.14, f32[2560]{0:T(1024)S(1)} %copy-done.29, f32[64]{0:T(128)S(1)} %add_sqrt_fusion), kind=kOutput, calls=%fused_computation.3 | convolution fusion | flops 420167680 | bytes 7055616 | tf_op jit(solution)/shard_map/dot_general | solution.py:513
  61.5 2.3 %collective-permute-start.10 = (bf16[16,2560]{1,0:T(8,128)(2,1)S(1)}, bf16[16,2560]{1,0:T(8,128)(2,1)S(1)}, u32[]{:S(2)}, u32[]{:S(2)}) collective-permute-start(bf16[16,2560]{1,0:T(8,128)(2,1)S(1)} %multiply_convert_fusion), channel_id=1, source_target_pairs={{0,24},{4,28},{8,16},{12,20},{16,8},{20,12},{24,0},{28,4},{1,25},{... | collective-permute-start | bytes 245768 | tf_op jit(solution)/shard_map/ppermute | solution.py:427
  63.8 2.1 %collective-permute-start.8 = (bf16[16,2560]{1,0:T(8,128)(2,1)S(1)}, bf16[16,2560]{1,0:T(8,128)(2,1)S(1)}, u32[]{:S(2)}, u32[]{:S(2)}) collective-permute-start(bf16[16,2560]{1,0:T(8,128)(2,1)S(1)} %multiply_convert_fusion), channel_id=1, source_target_pairs={{0,8},{4,12},{8,0},{12,4},{16,24},{20,28},{24,16},{28,20},{1,9},{5... | collective-permute-start | bytes 245768 | tf_op jit(solution)/shard_map/ppermute | solution.py:427
  66.9 3.6 %take_pieces.3 = (bf16[2,1280,128]{2,1,0:T(8,128)(2,1)}, bf16[2,1280,128]{2,1,0:T(8,128)(2,1)}, bf16[2,1280,128]{2,1,0:T(8,128)(2,1)}, bf16[2,1280,128]{2,1,0:T(8,128)(2,1)}, bf16[2,1280,128]{2,1,0:T(8,128)(2,1)}) custom-call(s32[16]{0:T(128)} %copy-done.10, s32[8]{0:T(128)} %iota_multiply_fusion.1.start, bf16[16,1280,128]{2,1,0:T(8,128)(2,1)} %bitcast.175), custom_call_target="tpu_custom_call" | custom-call | flops 1 | bytes 1 | tf_op jit(solution)/shard_map/take_pieces/pallas_call | solution.py:53
  71.7 3.6 %collective-permute-done.10 = bf16[16,2560]{1,0:T(8,128)(2,1)S(1)} collective-permute-done((bf16[16,2560]{1,0:T(8,128)(2,1)S(1)}, bf16[16,2560]{1,0:T(8,128)(2,1)S(1)}, u32[]{:S(2)}, u32[]{:S(2)}) %collective-permute-start.10) | collective-permute-done | bytes 81952 | tf_op jit(solution)/shard_map/ppermute | solution.py:427
  75.2 2.2 %collective-permute-start.7 = (bf16[2,1280,128]{2,1,0:T(8,128)(2,1)}, bf16[2,1280,128]{2,1,0:T(8,128)(2,1)}, u32[]{:S(2)}, u32[]{:S(2)}) collective-permute-start(bf16[2,1280,128]{2,1,0:T(8,128)(2,1)} %get-tuple-element.56), channel_id=1, source_target_pairs={{0,28},{4,24},{8,20},{12,16},{16,12},{20,8},{24,4},{28,0},{1,29},{... | collective-permute-start | bytes 1966088 | tf_op jit(solution)/shard_map/ppermute | solution.py:427
  77.5 1.6 collective-permute-start.11
  79.1 18.9 %collective-permute-done.11 = bf16[64,2560]{1,0:T(8,128)(2,1)S(1)} collective-permute-done((bf16[64,2560]{1,0:T(8,128)(2,1)S(1)}, bf16[64,2560]{1,0:T(8,128)(2,1)S(1)}, u32[]{:S(2)}, u32[]{:S(2)}) %collective-permute-start.11) | collective-permute-done | bytes 327712 | tf_op jit(solution)/shard_map/ppermute | solution.py:427
  98.1 1.4 fusion.115
  99.6 1.6 collective-permute-start.13
  102.1 14.2 %collective-permute-done.13 = bf16[128,2560]{1,0:T(8,128)(2,1)S(1)} collective-permute-done((bf16[128,2560]{1,0:T(8,128)(2,1)S(1)}, bf16[128,2560]{1,0:T(8,128)(2,1)S(1)}, u32[]{:S(2)}, u32[]{:S(2)}) %collective-permute-start.13) | collective-permute-done | bytes 655392 | tf_op jit(solution)/shard_map/ppermute | solution.py:427
  116.4 1.4 collective-permute-start.16
  117.9 28.5 %collective-permute-done.14.refs_5_ = bf16[2,1280,128]{2,1,0:T(8,128)(2,1)S(1)} collective-permute-done((bf16[2,1280,128]{2,1,0:T(8,128)(2,1)S(1)}, bf16[2,1280,128]{2,1,0:T(8,128)(2,1)S(1)}, u32[]{:S(2)}, u32[]{:S(2)}) %collective-permute-start.14) | collective-permute-done | bytes 655392 | tf_op jit(solution)/shard_map/ppermute | solution.py:427
  146.9 13.4 %collective-permute-done.16 = bf16[4,1280,128]{2,1,0:T(8,128)(2,1)S(1)} collective-permute-done((bf16[4,1280,128]{2,1,0:T(8,128)(2,1)S(1)}, bf16[4,1280,128]{2,1,0:T(8,128)(2,1)S(1)}, u32[]{:S(2)}, u32[]{:S(2)}) %collective-permute-start.16) | collective-permute-done | bytes 1310752 | tf_op jit(solution)/shard_map/ppermute | solution.py:427
  160.6 5.5 %head_logits.1 = (f32[1,512]{1,0:T(1,128)S(1)}, f32[1,512]{1,0:T(1,128)S(1)}) custom-call(s32[1]{0:T(128)} %bitcast.38.first, s32[1,512]{1,0:T(1,128)S(1)} %bitcast.170, bf16[512,2560]{1,0:T(8,128)(2,1)S(1)} %pad_maximum_fusion.final, bf16[1572,2560]{1,0:T(8,128)(2,1)S(1)} %bitcast.172), custom_call_target="tpu_custom_call" | custom-call | flops 4120903680 | bytes 8048640 | tf_op jit(solution)/shard_map/head_logits/pallas_call | solution.py:363
  167.8 1.6 collective-permute-start.19
  171.0 2.1 %collective-permute-done.20 = f32[3,8,16]{2,1,0:T(8,128)S(1)} collective-permute-done((f32[3,8,16]{2,1,0:T(8,128)S(1)}, f32[3,8,16]{2,1,0:T(8,128)S(1)}, u32[]{:S(2)}, u32[]{:S(2)}) %collective-permute-start.20) | collective-permute-done | bytes 1568 | tf_op jit(solution)/shard_map/ppermute | solution.py:427
  173.2 1.5 collective-permute-start.22
  176.8 1.1 copy-done.5
  177.9 1.1 copy-done.7
  179.0 7.3 %update_pieces.2.refs_1_ = bf16[16,1280,128]{2,1,0:T(8,128)(2,1)} custom-call(s32[16]{0:T(128)S(1)} %get-tuple-element.79.target, s32[8]{0:T(128)S(1)} %copy-done.12, f32[16,20]{1,0:T(8,128)S(1)} %get-tuple-element.137.keep, bf16[1280,128]{1,0:T(8,128)(2,1)S(1)} %bitcast.167, bf16[16,128,128]{2,1,0:T(8,128)(2,1)S(1)} %broadcast_select_fusion.writes, ...), custom_call_target="tpu_custom_call" | custom-call | tf_op jit(solution)/shard_map/update_pieces/pallas_call | solution.py:313
  187.7 3.1 %collective-permute-start.25 = (f32[3,16]{1,0:T(4,128)S(1)}, f32[3,16]{1,0:T(4,128)S(1)}, u32[]{:S(2)}, u32[]{:S(2)}) collective-permute-start(f32[3,16]{1,0:T(4,128)S(1)} %bitcast_maximum_fusion), channel_id=1, source_target_pairs={{0,24},{4,28},{8,16},{12,20},{16,8},{20,12},{24,0},{28,4},{1,25},{... | collective-permute-start | bytes 584 | tf_op jit(solution)/shard_map/ppermute | solution.py:427
  190.8 2.8 %update_pieces.3 = bf16[16,1280,128]{2,1,0:T(8,128)(2,1)} custom-call(s32[16]{0:T(128)S(1)} %get-tuple-element.79.target, s32[8]{0:T(128)S(1)} %copy-done.12, f32[16,20]{1,0:T(8,128)S(1)} %get-tuple-element.137.keep, bf16[1280,128]{1,0:T(8,128)(2,1)S(1)} %bitcast.168, ...), custom_call_target="tpu_custom_call", output_to_operand_aliasing={{}: (6, {})} | custom-call | tf_op jit(solution)/shard_map/update_pieces/pallas_call | solution.py:313
  (263 shorter events, 31.0 us)
Async XLA Ops:
  5.2 16.1 %collective-permute-start.2 = (bf16[2,12,2560]{2,1,0:T(8,128)(2,1)S(1)}, bf16[2,12,2560]{2,1,0:T(8,128)(2,1)S(1)}, u32[]{:S(2)}, u32[]{:S(2)}) collective-permute-start(bf16[2,12,2560]{2,1,0:T(8,128)(2,1)S(1)} %get-tuple-element.100), channel_id=1, source_target_pairs={{0,24},{4,28},{8,16},{12,20},{16,8},{20,12},{24,0},{28,4},{1,25},{... | collective-permute-start | bytes 368648 | tf_op jit(solution)/shard_map/ppermute | solution.py:427
  10.3 13.9 %collective-permute-start.1 = (bf16[2,12,2560]{2,1,0:T(8,128)(2,1)S(1)}, bf16[2,12,2560]{2,1,0:T(8,128)(2,1)S(1)}, u32[]{:S(2)}, u32[]{:S(2)}) collective-permute-start(bf16[2,12,2560]{2,1,0:T(8,128)(2,1)S(1)} %get-tuple-element.101), channel_id=1, source_target_pairs={{0,16},{4,20},{8,24},{12,28},{16,0},{20,4},{24,8},{28,12},{1,17},{... | collective-permute-start | bytes 368648 | tf_op jit(solution)/shard_map/ppermute | solution.py:427
  10.3 13.9 %collective-permute-start = (bf16[2,12,2560]{2,1,0:T(8,128)(2,1)S(1)}, bf16[2,12,2560]{2,1,0:T(8,128)(2,1)S(1)}, u32[]{:S(2)}, u32[]{:S(2)}) collective-permute-start(bf16[2,12,2560]{2,1,0:T(8,128)(2,1)S(1)} %get-tuple-element.102), channel_id=1, source_target_pairs={{0,8},{4,12},{8,0},{12,4},{16,24},{20,28},{24,16},{28,20},{1,9},{5... | collective-permute-start | bytes 368648 | tf_op jit(solution)/shard_map/ppermute | solution.py:427
  11.4 89.8 %copy-start.24 = (pred[16]{0:T(512)(128)(4,1)}, pred[16]{0:T(512)(128)(4,1)S(1)}, u32[]{:S(2)}) copy-start(pred[16]{0:T(512)(128)(4,1)S(1)} %get-tuple-element.160) | copy-start | bytes 52
  24.3 8.8 %collective-permute-start.3 = (bf16[4,12,2560]{2,1,0:T(8,128)(2,1)S(1)}, bf16[4,12,2560]{2,1,0:T(8,128)(2,1)S(1)}, u32[]{:S(2)}, u32[]{:S(2)}) collective-permute-start(bf16[4,12,2560]{2,1,0:T(8,128)(2,1)S(1)} %pad_maximum_fusion.4), channel_id=1, source_target_pairs={{0,4},{4,0},{8,12},{12,8},{16,20},{20,16},{24,28},{28,24},{1,5},{5... | collective-permute-start | bytes 737288 | tf_op jit(solution)/shard_map/ppermute | solution.py:427
  25.9 149.8 %collective-permute-start.18 = (bf16[2,1280,128]{2,1,0:T(8,128)(2,1)}, bf16[2,1280,128]{2,1,0:T(8,128)(2,1)}, u32[]{:S(2)}, u32[]{:S(2)}) collective-permute-start(bf16[2,1280,128]{2,1,0:T(8,128)(2,1)} %get-tuple-element.69), channel_id=1, source_target_pairs={{0,24},{4,28},{8,16},{12,20},{16,8},{20,12},{24,0},{28,4},{1,25},{... | collective-permute-start | bytes 1966088 | tf_op jit(solution)/shard_map/ppermute | solution.py:427
  28.4 69.7 %collective-permute-start.12 = (bf16[4,1280,128]{2,1,0:T(8,128)(2,1)}, bf16[4,1280,128]{2,1,0:T(8,128)(2,1)}, u32[]{:S(2)}, u32[]{:S(2)}) collective-permute-start(bf16[4,1280,128]{2,1,0:T(8,128)(2,1)} %get-tuple-element.59), channel_id=1, source_target_pairs={{0,8},{4,12},{8,0},{12,4},{16,24},{20,28},{24,16},{28,20},{1,9},{5... | collective-permute-start | bytes 3932168 | tf_op jit(solution)/shard_map/ppermute | solution.py:427
  48.8 4.1 %collective-permute-start.4 = (bf16[16,2816]{1,0:T(8,128)(2,1)S(1)}, bf16[16,2816]{1,0:T(8,128)(2,1)}, u32[]{:S(2)}, u32[]{:S(2)}) collective-permute-start(bf16[16,2816]{1,0:T(8,128)(2,1)S(1)} %get-tuple-element.108), channel_id=1, source_target_pairs={{0,1},{1,0},{2,3},{3,2},{4,5},{5,4},{6,7},{7,6},{8,9},{9,8},{10,11... | collective-permute-start | bytes 270344 | tf_op jit(solution)/shard_map/ppermute | solution.py:427
  48.9 4.9 %collective-permute-start.6 = (bf16[16,2816]{1,0:T(8,128)(2,1)S(1)}, bf16[16,2816]{1,0:T(8,128)(2,1)}, u32[]{:S(2)}, u32[]{:S(2)}) collective-permute-start(bf16[16,2816]{1,0:T(8,128)(2,1)S(1)} %get-tuple-element.109), channel_id=1, source_target_pairs={{0,3},{1,2},{2,1},{3,0},{4,7},{5,6},{6,5},{7,4},{8,11},{9,10},{10,... | collective-permute-start | bytes 270344 | tf_op jit(solution)/shard_map/ppermute | solution.py:427
  50.5 5.3 %collective-permute-start.5 = (bf16[16,2816]{1,0:T(8,128)(2,1)S(1)}, bf16[16,2816]{1,0:T(8,128)(2,1)S(1)}, u32[]{:S(2)}, u32[]{:S(2)}) collective-permute-start(bf16[16,2816]{1,0:T(8,128)(2,1)S(1)} %get-tuple-element.110), channel_id=1, source_target_pairs={{0,2},{1,3},{2,0},{3,1},{4,6},{5,7},{6,4},{7,5},{8,10},{9,11},{10,... | collective-permute-start | bytes 270344 | tf_op jit(solution)/shard_map/ppermute | solution.py:427
  61.5 13.8 %collective-permute-start.10 = (bf16[16,2560]{1,0:T(8,128)(2,1)S(1)}, bf16[16,2560]{1,0:T(8,128)(2,1)S(1)}, u32[]{:S(2)}, u32[]{:S(2)}) collective-permute-start(bf16[16,2560]{1,0:T(8,128)(2,1)S(1)} %multiply_convert_fusion), channel_id=1, source_target_pairs={{0,24},{4,28},{8,16},{12,20},{16,8},{20,12},{24,0},{28,4},{1,25},{... | collective-permute-start | bytes 245768 | tf_op jit(solution)/shard_map/ppermute | solution.py:427
  63.8 13.6 %collective-permute-start.9 = (bf16[16,2560]{1,0:T(8,128)(2,1)S(1)}, bf16[16,2560]{1,0:T(8,128)(2,1)S(1)}, u32[]{:S(2)}, u32[]{:S(2)}) collective-permute-start(bf16[16,2560]{1,0:T(8,128)(2,1)S(1)} %multiply_convert_fusion), channel_id=1, source_target_pairs={{0,16},{4,20},{8,24},{12,28},{16,0},{20,4},{24,8},{28,12},{1,17},{... | collective-permute-start | bytes 245768 | tf_op jit(solution)/shard_map/ppermute | solution.py:427
  63.8 13.6 %collective-permute-start.8 = (bf16[16,2560]{1,0:T(8,128)(2,1)S(1)}, bf16[16,2560]{1,0:T(8,128)(2,1)S(1)}, u32[]{:S(2)}, u32[]{:S(2)}) collective-permute-start(bf16[16,2560]{1,0:T(8,128)(2,1)S(1)} %multiply_convert_fusion), channel_id=1, source_target_pairs={{0,8},{4,12},{8,0},{12,4},{16,24},{20,28},{24,16},{28,20},{1,9},{5... | collective-permute-start | bytes 245768 | tf_op jit(solution)/shard_map/ppermute | solution.py:427
  71.0 27.0 %copy-start.44 = (bf16[2,1280,128]{2,1,0:T(8,128)(2,1)S(1)}, bf16[2,1280,128]{2,1,0:T(8,128)(2,1)}, u32[]{:S(2)}) copy-start(bf16[2,1280,128]{2,1,0:T(8,128)(2,1)} %get-tuple-element.66) | copy-start | bytes 1966084
  75.2 115.6 %collective-permute-start.7 = (bf16[2,1280,128]{2,1,0:T(8,128)(2,1)}, bf16[2,1280,128]{2,1,0:T(8,128)(2,1)}, u32[]{:S(2)}, u32[]{:S(2)}) collective-permute-start(bf16[2,1280,128]{2,1,0:T(8,128)(2,1)} %get-tuple-element.56), channel_id=1, source_target_pairs={{0,28},{4,24},{8,20},{12,16},{16,12},{20,8},{24,4},{28,0},{1,29},{... | collective-permute-start | bytes 1966088 | tf_op jit(solution)/shard_map/ppermute | solution.py:427
  77.4 69.0 %collective-permute-start.14 = (bf16[2,1280,128]{2,1,0:T(8,128)(2,1)S(1)}, bf16[2,1280,128]{2,1,0:T(8,128)(2,1)S(1)}, u32[]{:S(2)}, u32[]{:S(2)}) collective-permute-start(bf16[2,1280,128]{2,1,0:T(8,128)(2,1)S(1)} %copy-done.45), channel_id=1, source_target_pairs={{0,16},{4,20},{8,24},{12,28},{16,0},{20,4},{24,8},{28,12},{1,17},{... | collective-permute-start | bytes 1966088 | tf_op jit(solution)/shard_map/ppermute | solution.py:427
  77.5 20.5 %collective-permute-start.11 = (bf16[64,2560]{1,0:T(8,128)(2,1)S(1)}, bf16[64,2560]{1,0:T(8,128)(2,1)S(1)}, u32[]{:S(2)}, u32[]{:S(2)}) collective-permute-start(bf16[64,2560]{1,0:T(8,128)(2,1)S(1)} %pad_maximum_fusion.7), channel_id=1, source_target_pairs={{0,4},{4,0},{8,12},{12,8},{16,20},{20,16},{24,28},{28,24},{1,5},{5... | collective-permute-start | bytes 983048 | tf_op jit(solution)/shard_map/ppermute | solution.py:427
  98.0 68.1 %collective-permute-start.17 = (bf16[2,1280,128]{2,1,0:T(8,128)(2,1)S(1)}, bf16[2,1280,128]{2,1,0:T(8,128)(2,1)S(1)}, u32[]{:S(2)}, u32[]{:S(2)}) collective-permute-start(bf16[2,1280,128]{2,1,0:T(8,128)(2,1)S(1)} %copy-done.44), channel_id=1, source_target_pairs={{0,20},{4,16},{8,28},{12,24},{16,4},{20,0},{24,12},{28,8},{1,21},{... | collective-permute-start | bytes 1966088 | tf_op jit(solution)/shard_map/ppermute | solution.py:427
  99.5 61.0 %slice-start = ((s8[8069120]{0:T(1024)(128)(4,1)}), s8[4194304]{0:T(1024)(128)(4,1)S(1)}, s32[]{:S(2)}) async-start(s8[8069120]{0:T(1024)(128)(4,1)} %bitcast.171), calls=%async_computation | async-start | bytes 8388608
  99.6 16.7 %collective-permute-start.13 = (bf16[128,2560]{1,0:T(8,128)(2,1)S(1)}, bf16[128,2560]{1,0:T(8,128)(2,1)S(1)}, u32[]{:S(2)}, u32[]{:S(2)}) collective-permute-start(bf16[128,2560]{1,0:T(8,128)(2,1)S(1)} %constant_dynamic-update-slice_fusion), channel_id=1, source_target_pairs={{0,2},{1,3},{2,0},{3,1},{4,6},{5,7},{6,4},{7,5},{8,10},{9,11},{10,... | collective-permute-start | bytes 1966088 | tf_op jit(solution)/shard_map/ppermute | solution.py:427
  116.4 43.9 %collective-permute-start.16 = (bf16[4,1280,128]{2,1,0:T(8,128)(2,1)S(1)}, bf16[4,1280,128]{2,1,0:T(8,128)(2,1)S(1)}, u32[]{:S(2)}, u32[]{:S(2)}) collective-permute-start(bf16[4,1280,128]{2,1,0:T(8,128)(2,1)S(1)} %pad_maximum_fusion.1), channel_id=1, source_target_pairs={{0,4},{4,0},{8,12},{12,8},{16,20},{20,16},{24,28},{28,24},{1,5},{5... | collective-permute-start | bytes 3932168 | tf_op jit(solution)/shard_map/ppermute | solution.py:427
  117.9 28.6 %copy-start.30 = (pred[16,128]{1,0:T(8,128)(4,1)S(1)}, pred[16,128]{1,0:T(8,128)(4,1)}, u32[]{:S(2)}) copy-start(pred[16,128]{1,0:T(8,128)(4,1)} %iota_compare_fusion.7) | copy-start | bytes 6148
  146.4 14.0 %copy-start.4 = (bf16[2,1280,128]{2,1,0:T(8,128)(2,1)}, bf16[2,1280,128]{2,1,0:T(8,128)(2,1)S(1)}, u32[]{:S(2)}) copy-start(bf16[2,1280,128]{2,1,0:T(8,128)(2,1)S(1)} %collective-permute-done.14.refs_5_) | copy-start | bytes 1966084
  146.4 14.0 %collective-permute-start.15 = (bf16[256,2560]{1,0:T(8,128)(2,1)S(1)}, bf16[256,2560]{1,0:T(8,128)(2,1)S(1)}, u32[]{:S(2)}, u32[]{:S(2)}) collective-permute-start(bf16[256,2560]{1,0:T(8,128)(2,1)S(1)} %pad_maximum_fusion.2), channel_id=1, source_target_pairs={{0,1},{1,0},{2,3},{3,2},{4,5},{5,4},{6,7},{7,6},{8,9},{9,8},{10,11... | collective-permute-start | bytes 3932168 | tf_op jit(solution)/shard_map/ppermute | solution.py:427
  146.5 14.0 %slice-start.1 = ((s8[8069120]{0:T(1024)(128)(4,1)}), s8[3874816]{0:T(1024)(128)(4,1)S(1)}, s32[]{:S(2)}) async-start(s8[8069120]{0:T(1024)(128)(4,1)} %bitcast.171), calls=%async_computation.1 | async-start | bytes 7749632
  167.7 3.3 %collective-permute-start.21 = (f32[3,8,16]{2,1,0:T(8,128)S(1)}, f32[3,8,16]{2,1,0:T(8,128)S(1)}, u32[]{:S(2)}, u32[]{:S(2)}) collective-permute-start(f32[3,8,16]{2,1,0:T(8,128)S(1)} %bitcast.188), channel_id=1, source_target_pairs={{0,3},{1,2},{2,1},{3,0},{4,7},{5,6},{6,5},{7,4},{8,11},{9,10},{10,... | collective-permute-start | bytes 4616 | tf_op jit(solution)/shard_map/ppermute | solution.py:427
  167.8 3.2 %collective-permute-start.19 = (f32[3,8,16]{2,1,0:T(8,128)S(1)}, f32[3,8,16]{2,1,0:T(8,128)S(1)}, u32[]{:S(2)}, u32[]{:S(2)}) collective-permute-start(f32[3,8,16]{2,1,0:T(8,128)S(1)} %bitcast.187), channel_id=1, source_target_pairs={{0,1},{1,0},{2,3},{3,2},{4,5},{5,4},{6,7},{7,6},{8,9},{9,8},{10,11... | collective-permute-start | bytes 4616 | tf_op jit(solution)/shard_map/ppermute | solution.py:427
  169.4 3.7 %collective-permute-start.20 = (f32[3,8,16]{2,1,0:T(8,128)S(1)}, f32[3,8,16]{2,1,0:T(8,128)S(1)}, u32[]{:S(2)}, u32[]{:S(2)}) collective-permute-start(f32[3,8,16]{2,1,0:T(8,128)S(1)} %bitcast.186), channel_id=1, source_target_pairs={{0,2},{1,3},{2,0},{3,1},{4,6},{5,7},{6,4},{7,5},{8,10},{9,11},{10,... | collective-permute-start | bytes 4616 | tf_op jit(solution)/shard_map/ppermute | solution.py:427
  173.2 13.2 %collective-permute-start.22 = (f32[4,3,16]{2,0,1:T(4,128)S(1)}, f32[4,3,16]{2,0,1:T(4,128)S(1)}, u32[]{:S(2)}, u32[]{:S(2)}) collective-permute-start(f32[4,3,16]{2,0,1:T(4,128)S(1)} %pad_maximum_fusion.13), channel_id=1, source_target_pairs={{0,4},{4,0},{8,12},{12,8},{16,20},{20,16},{24,28},{28,24},{1,5},{5... | collective-permute-start | bytes 2312 | tf_op jit(solution)/shard_map/ppermute | solution.py:427
  186.4 7.3 %collective-permute-start.23 = (f32[3,16]{1,0:T(4,128)S(1)}, f32[3,16]{1,0:T(4,128)S(1)}, u32[]{:S(2)}, u32[]{:S(2)}) collective-permute-start(f32[3,16]{1,0:T(4,128)S(1)} %bitcast_maximum_fusion.2), channel_id=1, source_target_pairs={{0,8},{4,12},{8,0},{12,4},{16,24},{20,28},{24,16},{28,20},{1,9},{5... | collective-permute-start | bytes 584 | tf_op jit(solution)/shard_map/ppermute | solution.py:427
  186.7 6.9 %collective-permute-start.24 = (f32[3,16]{1,0:T(4,128)S(1)}, f32[3,16]{1,0:T(4,128)S(1)}, u32[]{:S(2)}, u32[]{:S(2)}) collective-permute-start(f32[3,16]{1,0:T(4,128)S(1)} %bitcast_maximum_fusion.1), channel_id=1, source_target_pairs={{0,16},{4,20},{8,24},{12,28},{16,0},{20,4},{24,8},{28,12},{1,17},{... | collective-permute-start | bytes 584 | tf_op jit(solution)/shard_map/ppermute | solution.py:427
  187.7 6.0 %collective-permute-start.25 = (f32[3,16]{1,0:T(4,128)S(1)}, f32[3,16]{1,0:T(4,128)S(1)}, u32[]{:S(2)}, u32[]{:S(2)}) collective-permute-start(f32[3,16]{1,0:T(4,128)S(1)} %bitcast_maximum_fusion), channel_id=1, source_target_pairs={{0,24},{4,28},{8,16},{12,20},{16,8},{20,12},{24,0},{28,4},{1,25},{... | collective-permute-start | bytes 584 | tf_op jit(solution)/shard_map/ppermute | solution.py:427
  (44 other events, 209.3 us)

commit v3 on v2

--- a/solution.py
+++ b/solution.py
@@ -273,17 +273,19 @@
     )(order, tokens, *small, *big, state)
 
 
-def update_body(where, size, heads, target, start, keep, weighted, writes, *refs):
+def update_body(where, heads, target, start, keep, weighted, writes, *refs):
     pieces = refs[: len(where)]
     out, before, after, arrive, leave = refs[-5:]
-    count = len(where) * size
+    steps = [(i, d, first, k) for i, (d, first, size) in enumerate(where) for k in range(size)]
+    count = len(steps)
 
     def at(index):
-        return start[where[index // size]] + index % size
+        _, distance, first, k = steps[index]
+        return start[distance] + first + k
 
     def read(index):
         return pltpu.make_async_copy(
-            pieces[index // size].at[index % size], before.at[index], arrive.at[index]
+            pieces[steps[index][0]].at[steps[index][3]], before.at[index], arrive.at[index]
         )
 
     def write(index):
@@ -307,11 +309,12 @@
 
 
 def update_pieces(target, start, keep, weighted, writes, where, pieces, whole):
-    size, width, state_dim = pieces[0].shape
+    width, state_dim = pieces[0].shape[1:]
     req_dev, heads = keep.shape
-    count = len(where) * size
+    where = [(d, first, piece.shape[0]) for (d, first), piece in zip(where, pieces)]
+    count = sum(size for _, _, size in where)
     return pl.pallas_call(
-        functools.partial(update_body, tuple(where), size, heads),
+        functools.partial(update_body, tuple(where), heads),
         grid_spec=pltpu.PrefetchScalarGridSpec(
             num_scalar_prefetch=3,
             grid=(),
@@ -583,7 +586,7 @@
         home_row_b, start, states, [(0,), (1,)] + [(d,) for d in phases[1]], each
     )
     arrived[0] = local
-    for d, value in zip(phases[1], leaving_b):
+    for d, value in zip(phases[1][:1], leaving_b):
         arrived[d] = swap(value, "req", d)
     everyone = final
     for step, (axis, masks) in enumerate((
@@ -603,6 +606,13 @@
             everyone, passed_on = lax.optimization_barrier((everyone, passed_on))
             passed_on = swap(passed_on, "req", 1)
             arrived[1], arrived[3] = passed_on[:each], passed_on[each:]
+        if step in (1, 2):
+            some = slice(1, 2) if step == 1 else slice(2, None)
+            everyone, *going = lax.optimization_barrier((everyone, *leaving_b[some]))
+            for d, value in zip(phases[1][some], going):
+                cuts = (0, each) if step == 1 or each == 1 else (0, each // 2, each)
+                parts = [swap(value[i:j], "req", d) for i, j in zip(cuts, cuts[1:])]
+                arrived[d] = list(zip(cuts, parts)) if step == 2 else parts[0]
         unit = n_head if axis == "req" else 1
         distance = distance + [e ^ (m * unit) for m in masks for e in distance]
 
@@ -621,7 +631,7 @@
     ids_here = jnp.sum(jnp.where(pick, draft_ids[:, None], 0), axis=0)
     first_row = jnp.full((1,), my_device * vocab_dev, i32)
     top, draft = head_logits(first_row, ids_here[None, :], everyone, embedding)
-    held = [1, 3] + phases[1][1:2]
+    held = [1, 3]
     top, draft, *values = lax.optimization_barrier((top, draft, *(arrived[d] for d in held)))
     arrived.update(zip(held, values))
     scales = jnp.concatenate([scale[:, 0], jnp.full((tokens - share,), lowest, f32)])
@@ -641,6 +651,12 @@
         return lax.dynamic_index_in_dim(best, req_index ^ distance, axis=1, keepdims=False)
 
     far = swap(jnp.stack([for_req(mask ^ 1) for mask in range(0, n_req, 2)]), "req", 1)
+    for d in phases[1][2:]:
+        first, part = arrived[d][0]
+        far, part = lax.optimization_barrier((far, part))
+        arrived[d][0] = (first, part)
+    for d in phases[1][1:2]:
+        far, arrived[d] = lax.optimization_barrier((far, arrived[d]))
     own = jnp.maximum(for_req(0), far[0])
     for mask in range(2, n_req, 2):
         own = jnp.maximum(own, swap(jnp.maximum(for_req(mask), far[mask // 2]), "req", mask))
@@ -689,9 +705,10 @@
 
     update = functools.partial(update_pieces, target, start, keep, weighted, writes)
     early = [0, 1, 2, 3] + phases[0] + phases[1][:2]
-    after = update(early, [arrived[d] for d in early], ())
-    late = phases[1][2:]
-    after = update(late, [arrived[d] for d in late], (after,))
+    after = update([(d, 0) for d in early], [arrived[d] for d in early], ())
+    last = phases[1][2:]
+    late = [(d, first) for d in last for first, _ in arrived[d]]
+    after = update(late, [part for d in last for _, part in arrived[d]], (after,))
     state_after = after.reshape(state_cache.shape)
     top_logit, draft_logit, hidden_rms = own
     return (state_after, tail_inner, tail_readwrite, hidden_rms, top_logit, draft_logit)

time: 195 us -> 174 us (0.89)
  waiting for transfers between devices: 90.3 us -> 64.9 us
  starting transfers between devices: 31.3 us -> 36.2 us
    ppermute x26 -> x27, waiting for transfers between devices: 90.3 us -> 64.9 us  [swap(): lax.ppermute(values, axis, [(i, i ^ mask) for i in range(lax.axis_size(ax...]
    ppermute x26 -> x27, starting transfers between devices: 31.3 us -> 36.2 us  [swap(): lax.ppermute(values, axis, [(i, i ^ mask) for i in range(lax.axis_size(ax...]
    unnamed x105 -> x95, local copies, waits for them, and re-layouts: 6.32 us -> 4.32 us
    slice x0 -> x1, local copies, waits for them, and re-layouts: none -> 1.98 us  [on_device(): parts = [swap(value[i:j], 'req', d) for i, j in zip(cuts, cuts[1:])]]
  transfers between devices with their start and end apart: 26 -> 27, of which waited for: 10 -> 12; matrix products, arithmetic and copies ran while one was open for 12% -> 15% of each run, Pallas kernels for 18% -> 20%
where the time goes in v3:
time: 174 us
  waiting for transfers between devices  64.9 us (37%)
  starting transfers between devices  36.2 us (21%)
  Pallas kernels  35.2 us (20%)
  local copies, waits for them, and re-layouts  13.9 us (8%)
  other arithmetic  12.2 us (7%)
  matrix products  9.19 us (5%)
  between operations  1.96 us (1%)
    ppermute x27, waiting for transfers between devices, swap(): lax.ppermute(values, axis, [(i, i ^ mask) for i in range(lax.axis_size(ax...  64.9 us
    ppermute x27, starting transfers between devices, swap(): lax.ppermute(values, axis, [(i, i ^ mask) for i in range(lax.axis_size(ax...  36.2 us
    pallas_call x1, Pallas kernels, home_tokens(): pl.pallas_call(functools.partial(home_body, (requests, slots, state_dim,...  13.5 us
    pallas_call x2, Pallas kernels, update_pieces(): pl.pallas_call(functools.partial(update_body, tuple(where), heads), grid_...  9.5 us
    pallas_call x2, Pallas kernels, take_pieces(): pl.pallas_call(functools.partial(pieces_body, tuple(where), size), grid_s...  6.68 us
    pallas_call x1, Pallas kernels, head_logits(): pl.pallas_call(functools.partial(head_body, vocab), grid_spec=pltpu.Prefe...  5.5 us
    unnamed x95, local copies, waits for them, and re-layouts  4.32 us
    dot_general x1, matrix products, project(): jnp.dot(normed, inner_weight, preferred_element_type=f32).astype(bf16)  4.2 us
  transfers between devices with their start and end apart: 27, of which 12 were waited for; matrix products, arithmetic and copies ran while one was open for 15% of the time, Pallas kernels for 20%

profile of v3, /device:TPU:0, one launch (start us, length us, event | category | flops | bytes accessed | tf_op | source)
XLA Modules:
  0.0 173.6 jit_solution(10462082656560386422)
XLA Ops:
  2.9 1.1 fusion.old_inner
  5.2 5.0 %collective-permute-start.2 = (bf16[2,12,2560]{2,1,0:T(8,128)(2,1)S(1)}, bf16[2,12,2560]{2,1,0:T(8,128)(2,1)S(1)}, u32[]{:S(2)}, u32[]{:S(2)}) collective-permute-start(bf16[2,12,2560]{2,1,0:T(8,128)(2,1)S(1)} %get-tuple-element.116), channel_id=1, source_target_pairs={{0,24},{4,28},{8,16},{12,20},{16,8},{20,12},{24,0},{28,4},{1,25},{... | collective-permute-start | bytes 368648 | tf_op jit(solution)/shard_map/ppermute | solution.py:430
  16.1 3.2 %take_pieces.2 = (bf16[4,1280,128]{2,1,0:T(8,128)(2,1)}, bf16[2,1280,128]{2,1,0:T(8,128)(2,1)}) custom-call(s32[16]{0:T(128)} %copy-done.8, s32[8]{0:T(128)} %iota_multiply_fusion.1.start, bf16[16,1280,128]{2,1,0:T(8,128)(2,1)} %bitcast.173), custom_call_target="tpu_custom_call" | custom-call | flops 1 | bytes 1 | tf_op jit(solution)/shard_map/take_pieces/pallas_call | solution.py:53
  21.3 2.8 %collective-permute-done.1 = bf16[2,12,2560]{2,1,0:T(8,128)(2,1)S(1)} collective-permute-done((bf16[2,12,2560]{2,1,0:T(8,128)(2,1)S(1)}, bf16[2,12,2560]{2,1,0:T(8,128)(2,1)S(1)}, u32[]{:S(2)}, u32[]{:S(2)}) %collective-permute-start.1) | collective-permute-done | bytes 122912 | tf_op jit(solution)/shard_map/ppermute | solution.py:430
  24.3 1.6 collective-permute-start.3
  25.9 2.5 %collective-permute-start.22 = (bf16[2,1280,128]{2,1,0:T(8,128)(2,1)}, bf16[2,1280,128]{2,1,0:T(8,128)(2,1)}, u32[]{:S(2)}, u32[]{:S(2)}) collective-permute-start(bf16[2,1280,128]{2,1,0:T(8,128)(2,1)} %get-tuple-element.82), channel_id=1, source_target_pairs={{0,24},{4,28},{8,16},{12,20},{16,8},{20,12},{24,0},{28,4},{1,25},{... | collective-permute-start | bytes 1966088 | tf_op jit(solution)/shard_map/ppermute | solution.py:430
  28.4 4.7 %collective-permute-done.3 = bf16[4,12,2560]{2,1,0:T(8,128)(2,1)S(1)} collective-permute-done((bf16[4,12,2560]{2,1,0:T(8,128)(2,1)S(1)}, bf16[4,12,2560]{2,1,0:T(8,128)(2,1)S(1)}, u32[]{:S(2)}, u32[]{:S(2)}) %collective-permute-start.3) | collective-permute-done | bytes 245792 | tf_op jit(solution)/shard_map/ppermute | solution.py:430
  35.2 13.5 %home_tokens.1 = (bf16[64,2816]{1,0:T(8,128)(2,1)S(1)}, f32[64,2560]{1,0:T(8,128)S(1)}, f32[64,128]{1,0:T(8,128)S(1)}, bf16[64,2560]{1,0:T(8,128)(2,1)S(1)}) custom-call(s32[16]{0:T(128)S(1)} %copy-done.9, bf16[64,2560]{1,0:T(8,128)(2,1)S(1)} %bitcast.169, f32[1,2560]{1,0:T(1,128)S(1)} %broadcast_in_dim.304.norm_gain, ...), custom_call_target="tpu_custom_call" | custom-call | flops 1 | bytes 1 | tf_op jit(solution)/shard_map/home_tokens/pallas_call | solution.py:248
  48.9 1.6 collective-permute-start.6
  57.3 4.2 %convolution_convert_fusion.1 = bf16[64,1280]{1,0:T(8,128)(2,1)S(1)} fusion(bf16[2560,1280]{1,0:T(8,128)(2,1)} %weights_inner.1, bf16[64,2560]{1,0:T(8,128)(2,1)S(1)} %copy-done.12, f32[2560]{0:T(1024)S(1)} %copy-done.25, f32[64]{0:T(128)S(1)} %add_sqrt_fusion), kind=kOutput, calls=%fused_computation.3 | convolution fusion | flops 420167680 | bytes 7055616 | tf_op jit(solution)/shard_map/dot_general | solution.py:516
  61.5 2.3 %collective-permute-start.9 = (bf16[16,2560]{1,0:T(8,128)(2,1)S(1)}, bf16[16,2560]{1,0:T(8,128)(2,1)S(1)}, u32[]{:S(2)}, u32[]{:S(2)}) collective-permute-start(bf16[16,2560]{1,0:T(8,128)(2,1)S(1)} %multiply_convert_fusion), channel_id=1, source_target_pairs={{0,24},{4,28},{8,16},{12,20},{16,8},{20,12},{24,0},{28,4},{1,25},{... | collective-permute-start | bytes 245768 | tf_op jit(solution)/shard_map/ppermute | solution.py:430
  63.8 2.1 %collective-permute-start.7 = (bf16[16,2560]{1,0:T(8,128)(2,1)S(1)}, bf16[16,2560]{1,0:T(8,128)(2,1)S(1)}, u32[]{:S(2)}, u32[]{:S(2)}) collective-permute-start(bf16[16,2560]{1,0:T(8,128)(2,1)S(1)} %multiply_convert_fusion), channel_id=1, source_target_pairs={{0,8},{4,12},{8,0},{12,4},{16,24},{20,28},{24,16},{28,20},{1,9},{5... | collective-permute-start | bytes 245768 | tf_op jit(solution)/shard_map/ppermute | solution.py:430
  69.4 3.5 %take_pieces.3 = (bf16[2,1280,128]{2,1,0:T(8,128)(2,1)}, bf16[2,1280,128]{2,1,0:T(8,128)(2,1)}, bf16[2,1280,128]{2,1,0:T(8,128)(2,1)}, bf16[2,1280,128]{2,1,0:T(8,128)(2,1)}, bf16[2,1280,128]{2,1,0:T(8,128)(2,1)}) custom-call(s32[16]{0:T(128)} %copy-done.8, s32[8]{0:T(128)} %iota_multiply_fusion.1.start, bf16[16,1280,128]{2,1,0:T(8,128)(2,1)} %bitcast.175), custom_call_target="tpu_custom_call" | custom-call | flops 1 | bytes 1 | tf_op jit(solution)/shard_map/take_pieces/pallas_call | solution.py:53
  72.9 2.3 %collective-permute-done.9 = bf16[16,2560]{1,0:T(8,128)(2,1)S(1)} collective-permute-done((bf16[16,2560]{1,0:T(8,128)(2,1)S(1)}, bf16[16,2560]{1,0:T(8,128)(2,1)S(1)}, u32[]{:S(2)}, u32[]{:S(2)}) %collective-permute-start.9) | collective-permute-done | bytes 81952 | tf_op jit(solution)/shard_map/ppermute | solution.py:430
  75.2 2.0 %collective-permute-done.7 = bf16[16,2560]{1,0:T(8,128)(2,1)S(1)} collective-permute-done((bf16[16,2560]{1,0:T(8,128)(2,1)S(1)}, bf16[16,2560]{1,0:T(8,128)(2,1)S(1)}, u32[]{:S(2)}, u32[]{:S(2)}) %collective-permute-start.7) | collective-permute-done | bytes 81952 | tf_op jit(solution)/shard_map/ppermute | solution.py:430
  77.7 9.1 %collective-permute-done.10 = bf16[64,2560]{1,0:T(8,128)(2,1)S(1)} collective-permute-done((bf16[64,2560]{1,0:T(8,128)(2,1)S(1)}, bf16[64,2560]{1,0:T(8,128)(2,1)S(1)}, u32[]{:S(2)}, u32[]{:S(2)}) %collective-permute-start.10) | collective-permute-done | bytes 327712 | tf_op jit(solution)/shard_map/ppermute | solution.py:430
  86.9 1.4 fusion.115
  88.5 1.6 collective-permute-start.12
  90.7 13.5 %collective-permute-done.12 = bf16[128,2560]{1,0:T(8,128)(2,1)S(1)} collective-permute-done((bf16[128,2560]{1,0:T(8,128)(2,1)S(1)}, bf16[128,2560]{1,0:T(8,128)(2,1)S(1)}, u32[]{:S(2)}, u32[]{:S(2)}) %collective-permute-start.12) | collective-permute-done | bytes 655392 | tf_op jit(solution)/shard_map/ppermute | solution.py:430
  105.0 14.8 %collective-permute-done.15 = bf16[4,1280,128]{2,1,0:T(8,128)(2,1)S(1)} collective-permute-done((bf16[4,1280,128]{2,1,0:T(8,128)(2,1)S(1)}, bf16[4,1280,128]{2,1,0:T(8,128)(2,1)S(1)}, u32[]{:S(2)}, u32[]{:S(2)}) %collective-permute-start.15) | collective-permute-done | bytes 1310752 | tf_op jit(solution)/shard_map/ppermute | solution.py:430
  120.1 5.5 %head_logits.1 = (f32[1,512]{1,0:T(1,128)S(1)}, f32[1,512]{1,0:T(1,128)S(1)}) custom-call(s32[1]{0:T(128)} %bitcast.38.first, s32[1,512]{1,0:T(1,128)S(1)} %bitcast.170, bf16[512,2560]{1,0:T(8,128)(2,1)S(1)} %pad_maximum_fusion.final, bf16[1572,2560]{1,0:T(8,128)(2,1)S(1)} %bitcast.172), custom_call_target="tpu_custom_call" | custom-call | flops 4120903680 | bytes 8048640 | tf_op jit(solution)/shard_map/head_logits/pallas_call | solution.py:366
  127.0 1.5 collective-permute-start.17
  128.6 2.0 %fusion.117 = (bf16[1,1280,128]{2,1,0:T(8,128)(2,1)}, bf16[1,1280,128]{2,1,0:T(8,128)(2,1)}) fusion(bf16[2,1280,128]{2,1,0:T(8,128)(2,1)} %get-tuple-element.77), kind=kLoop, calls=%fused_computation.305 | loop fusion | bytes 1310720 | tf_op jit(solution)/shard_map/slice | solution.py:614
  130.8 1.4 collective-permute-start.19
  133.3 3.6 %collective-permute-start.21 = (bf16[1,1280,128]{2,1,0:T(8,128)(2,1)}, bf16[1,1280,128]{2,1,0:T(8,128)(2,1)S(1)}, u32[]{:S(2)}, u32[]{:S(2)}) collective-permute-start(bf16[1,1280,128]{2,1,0:T(8,128)(2,1)} %get-tuple-element.114), channel_id=1, source_target_pairs={{0,28},{4,24},{8,20},{12,16},{16,12},{20,8},{24,4},{28,0},{1,29},{... | collective-permute-start | bytes 983048 | tf_op jit(solution)/shard_map/ppermute | solution.py:430
  136.9 7.3 %collective-permute-done.20.refs_0_ = bf16[1,1280,128]{2,1,0:T(8,128)(2,1)S(1)} collective-permute-done((bf16[1,1280,128]{2,1,0:T(8,128)(2,1)}, bf16[1,1280,128]{2,1,0:T(8,128)(2,1)S(1)}, u32[]{:S(2)}, u32[]{:S(2)}) %collective-permute-start.20) | collective-permute-done | bytes 327712 | tf_op jit(solution)/shard_map/ppermute | solution.py:430
  144.2 7.0 %collective-permute-done.19 = f32[4,3,16]{2,0,1:T(4,128)S(1)} collective-permute-done((f32[4,3,16]{2,0,1:T(4,128)S(1)}, f32[4,3,16]{2,0,1:T(4,128)S(1)}, u32[]{:S(2)}, u32[]{:S(2)}) %collective-permute-start.19) | collective-permute-done | bytes 800 | tf_op jit(solution)/shard_map/ppermute | solution.py:430
  151.4 7.5 %collective-permute-start.24 = (f32[3,16]{1,0:T(4,128)S(1)}, f32[3,16]{1,0:T(4,128)S(1)}, u32[]{:S(2)}, u32[]{:S(2)}) collective-permute-start(f32[3,16]{1,0:T(4,128)S(1)} %bitcast_maximum_fusion.2), channel_id=1, source_target_pairs={{0,8},{4,12},{8,0},{12,4},{16,24},{20,28},{24,16},{28,20},{1,9},{5... | collective-permute-start | bytes 584 | tf_op jit(solution)/shard_map/ppermute | solution.py:430
  159.0 2.3 %collective-permute-start.26 = (f32[3,16]{1,0:T(4,128)S(1)}, f32[3,16]{1,0:T(4,128)S(1)}, u32[]{:S(2)}, u32[]{:S(2)}) collective-permute-start(f32[3,16]{1,0:T(4,128)S(1)} %bitcast_maximum_fusion), channel_id=1, source_target_pairs={{0,24},{4,28},{8,16},{12,20},{16,8},{20,12},{24,0},{28,4},{1,25},{... | collective-permute-start | bytes 584 | tf_op jit(solution)/shard_map/ppermute | solution.py:430
  161.3 1.1 copy-done.3
  163.5 7.1 %update_pieces.2.refs_2_ = bf16[16,1280,128]{2,1,0:T(8,128)(2,1)} custom-call(s32[16]{0:T(128)S(1)} %get-tuple-element.93.target, s32[8]{0:T(128)S(1)} %copy-done.10, f32[16,20]{1,0:T(8,128)S(1)} %get-tuple-element.153.keep, bf16[1280,128]{1,0:T(8,128)(2,1)S(1)} %bitcast.167, bf16[16,128,128]{2,1,0:T(8,128)(2,1)S(1)} %broadcast_select_fusion.writes, ...), custom_call_target="tpu_custom_call" | custom-call | tf_op jit(solution)/shard_map/update_pieces/pallas_call | solution.py:316
  170.7 2.4 %update_pieces.3 = bf16[16,1280,128]{2,1,0:T(8,128)(2,1)} custom-call(s32[16]{0:T(128)S(1)} %get-tuple-element.93.target, s32[8]{0:T(128)S(1)} %copy-done.10, f32[16,20]{1,0:T(8,128)S(1)} %get-tuple-element.153.keep, bf16[1280,128]{1,0:T(8,128)(2,1)S(1)} %bitcast.168, ...), custom_call_target="tpu_custom_call", output_to_operand_aliasing={{}: (7, {})} | custom-call | tf_op jit(solution)/shard_map/update_pieces/pallas_call | solution.py:316
  (256 shorter events, 29.9 us)
Async XLA Ops:
  5.2 16.1 %collective-permute-start.2 = (bf16[2,12,2560]{2,1,0:T(8,128)(2,1)S(1)}, bf16[2,12,2560]{2,1,0:T(8,128)(2,1)S(1)}, u32[]{:S(2)}, u32[]{:S(2)}) collective-permute-start(bf16[2,12,2560]{2,1,0:T(8,128)(2,1)S(1)} %get-tuple-element.116), channel_id=1, source_target_pairs={{0,24},{4,28},{8,16},{12,20},{16,8},{20,12},{24,0},{28,4},{1,25},{... | collective-permute-start | bytes 368648 | tf_op jit(solution)/shard_map/ppermute | solution.py:430
  10.3 13.9 %collective-permute-start.1 = (bf16[2,12,2560]{2,1,0:T(8,128)(2,1)S(1)}, bf16[2,12,2560]{2,1,0:T(8,128)(2,1)S(1)}, u32[]{:S(2)}, u32[]{:S(2)}) collective-permute-start(bf16[2,12,2560]{2,1,0:T(8,128)(2,1)S(1)} %get-tuple-element.117), channel_id=1, source_target_pairs={{0,16},{4,20},{8,24},{12,28},{16,0},{20,4},{24,8},{28,12},{1,17},{... | collective-permute-start | bytes 368648 | tf_op jit(solution)/shard_map/ppermute | solution.py:430
  10.3 13.9 %collective-permute-start = (bf16[2,12,2560]{2,1,0:T(8,128)(2,1)S(1)}, bf16[2,12,2560]{2,1,0:T(8,128)(2,1)S(1)}, u32[]{:S(2)}, u32[]{:S(2)}) collective-permute-start(bf16[2,12,2560]{2,1,0:T(8,128)(2,1)S(1)} %get-tuple-element.118), channel_id=1, source_target_pairs={{0,8},{4,12},{8,0},{12,4},{16,24},{20,28},{24,16},{28,20},{1,9},{5... | collective-permute-start | bytes 368648 | tf_op jit(solution)/shard_map/ppermute | solution.py:430
  24.3 8.8 %collective-permute-start.3 = (bf16[4,12,2560]{2,1,0:T(8,128)(2,1)S(1)}, bf16[4,12,2560]{2,1,0:T(8,128)(2,1)S(1)}, u32[]{:S(2)}, u32[]{:S(2)}) collective-permute-start(bf16[4,12,2560]{2,1,0:T(8,128)(2,1)S(1)} %pad_maximum_fusion.4), channel_id=1, source_target_pairs={{0,4},{4,0},{8,12},{12,8},{16,20},{20,16},{24,28},{28,24},{1,5},{5... | collective-permute-start | bytes 737288 | tf_op jit(solution)/shard_map/ppermute | solution.py:430
  25.9 135.4 %collective-permute-start.22 = (bf16[2,1280,128]{2,1,0:T(8,128)(2,1)}, bf16[2,1280,128]{2,1,0:T(8,128)(2,1)}, u32[]{:S(2)}, u32[]{:S(2)}) collective-permute-start(bf16[2,1280,128]{2,1,0:T(8,128)(2,1)} %get-tuple-element.82), channel_id=1, source_target_pairs={{0,24},{4,28},{8,16},{12,20},{16,8},{20,12},{24,0},{28,4},{1,25},{... | collective-permute-start | bytes 1966088 | tf_op jit(solution)/shard_map/ppermute | solution.py:430
  28.4 58.5 %collective-permute-start.11 = (bf16[4,1280,128]{2,1,0:T(8,128)(2,1)}, bf16[4,1280,128]{2,1,0:T(8,128)(2,1)}, u32[]{:S(2)}, u32[]{:S(2)}) collective-permute-start(bf16[4,1280,128]{2,1,0:T(8,128)(2,1)} %get-tuple-element.64), channel_id=1, source_target_pairs={{0,8},{4,12},{8,0},{12,4},{16,24},{20,28},{24,16},{28,20},{1,9},{5... | collective-permute-start | bytes 3932168 | tf_op jit(solution)/shard_map/ppermute | solution.py:430
  48.8 4.1 %collective-permute-start.4 = (bf16[16,2816]{1,0:T(8,128)(2,1)S(1)}, bf16[16,2816]{1,0:T(8,128)(2,1)}, u32[]{:S(2)}, u32[]{:S(2)}) collective-permute-start(bf16[16,2816]{1,0:T(8,128)(2,1)S(1)} %get-tuple-element.124), channel_id=1, source_target_pairs={{0,1},{1,0},{2,3},{3,2},{4,5},{5,4},{6,7},{7,6},{8,9},{9,8},{10,11... | collective-permute-start | bytes 270344 | tf_op jit(solution)/shard_map/ppermute | solution.py:430
  48.9 4.9 %collective-permute-start.6 = (bf16[16,2816]{1,0:T(8,128)(2,1)S(1)}, bf16[16,2816]{1,0:T(8,128)(2,1)}, u32[]{:S(2)}, u32[]{:S(2)}) collective-permute-start(bf16[16,2816]{1,0:T(8,128)(2,1)S(1)} %get-tuple-element.125), channel_id=1, source_target_pairs={{0,3},{1,2},{2,1},{3,0},{4,7},{5,6},{6,5},{7,4},{8,11},{9,10},{10,... | collective-permute-start | bytes 270344 | tf_op jit(solution)/shard_map/ppermute | solution.py:430
  50.5 5.3 %collective-permute-start.5 = (bf16[16,2816]{1,0:T(8,128)(2,1)S(1)}, bf16[16,2816]{1,0:T(8,128)(2,1)S(1)}, u32[]{:S(2)}, u32[]{:S(2)}) collective-permute-start(bf16[16,2816]{1,0:T(8,128)(2,1)S(1)} %get-tuple-element.126), channel_id=1, source_target_pairs={{0,2},{1,3},{2,0},{3,1},{4,6},{5,7},{6,4},{7,5},{8,10},{9,11},{10,... | collective-permute-start | bytes 270344 | tf_op jit(solution)/shard_map/ppermute | solution.py:430
  61.5 13.7 %collective-permute-start.9 = (bf16[16,2560]{1,0:T(8,128)(2,1)S(1)}, bf16[16,2560]{1,0:T(8,128)(2,1)S(1)}, u32[]{:S(2)}, u32[]{:S(2)}) collective-permute-start(bf16[16,2560]{1,0:T(8,128)(2,1)S(1)} %multiply_convert_fusion), channel_id=1, source_target_pairs={{0,24},{4,28},{8,16},{12,20},{16,8},{20,12},{24,0},{28,4},{1,25},{... | collective-permute-start | bytes 245768 | tf_op jit(solution)/shard_map/ppermute | solution.py:430
  63.8 11.4 %collective-permute-start.8 = (bf16[16,2560]{1,0:T(8,128)(2,1)S(1)}, bf16[16,2560]{1,0:T(8,128)(2,1)S(1)}, u32[]{:S(2)}, u32[]{:S(2)}) collective-permute-start(bf16[16,2560]{1,0:T(8,128)(2,1)S(1)} %multiply_convert_fusion), channel_id=1, source_target_pairs={{0,16},{4,20},{8,24},{12,28},{16,0},{20,4},{24,8},{28,12},{1,17},{... | collective-permute-start | bytes 245768 | tf_op jit(solution)/shard_map/ppermute | solution.py:430
  63.8 13.4 %collective-permute-start.7 = (bf16[16,2560]{1,0:T(8,128)(2,1)S(1)}, bf16[16,2560]{1,0:T(8,128)(2,1)S(1)}, u32[]{:S(2)}, u32[]{:S(2)}) collective-permute-start(bf16[16,2560]{1,0:T(8,128)(2,1)S(1)} %multiply_convert_fusion), channel_id=1, source_target_pairs={{0,8},{4,12},{8,0},{12,4},{16,24},{20,28},{24,16},{28,20},{1,9},{5... | collective-permute-start | bytes 245768 | tf_op jit(solution)/shard_map/ppermute | solution.py:430
  75.2 29.1 %collective-permute-start.13 = (bf16[2,1280,128]{2,1,0:T(8,128)(2,1)}, bf16[2,1280,128]{2,1,0:T(8,128)(2,1)S(1)}, u32[]{:S(2)}, u32[]{:S(2)}) collective-permute-start(bf16[2,1280,128]{2,1,0:T(8,128)(2,1)} %get-tuple-element.70), channel_id=1, source_target_pairs={{0,16},{4,20},{8,24},{12,28},{16,0},{20,4},{24,8},{28,12},{1,17},{... | collective-permute-start | bytes 1966088 | tf_op jit(solution)/shard_map/ppermute | solution.py:430
  77.2 9.6 %collective-permute-start.10 = (bf16[64,2560]{1,0:T(8,128)(2,1)S(1)}, bf16[64,2560]{1,0:T(8,128)(2,1)S(1)}, u32[]{:S(2)}, u32[]{:S(2)}) collective-permute-start(bf16[64,2560]{1,0:T(8,128)(2,1)S(1)} %pad_maximum_fusion.7), channel_id=1, source_target_pairs={{0,4},{4,0},{8,12},{12,8},{16,20},{20,16},{24,28},{28,24},{1,5},{5... | collective-permute-start | bytes 983048 | tf_op jit(solution)/shard_map/ppermute | solution.py:430
  88.3 31.7 %slice-start = ((s8[8069120]{0:T(1024)(128)(4,1)}), s8[4194304]{0:T(1024)(128)(4,1)S(1)}, s32[]{:S(2)}) async-start(s8[8069120]{0:T(1024)(128)(4,1)} %bitcast.171), calls=%async_computation | async-start | bytes 8388608
  88.5 15.8 %collective-permute-start.12 = (bf16[128,2560]{1,0:T(8,128)(2,1)S(1)}, bf16[128,2560]{1,0:T(8,128)(2,1)S(1)}, u32[]{:S(2)}, u32[]{:S(2)}) collective-permute-start(bf16[128,2560]{1,0:T(8,128)(2,1)S(1)} %constant_dynamic-update-slice_fusion), channel_id=1, source_target_pairs={{0,2},{1,3},{2,0},{3,1},{4,6},{5,7},{6,4},{7,5},{8,10},{9,11},{10,... | collective-permute-start | bytes 1966088 | tf_op jit(solution)/shard_map/ppermute | solution.py:430
  90.2 29.6 %collective-permute-start.15 = (bf16[4,1280,128]{2,1,0:T(8,128)(2,1)S(1)}, bf16[4,1280,128]{2,1,0:T(8,128)(2,1)S(1)}, u32[]{:S(2)}, u32[]{:S(2)}) collective-permute-start(bf16[4,1280,128]{2,1,0:T(8,128)(2,1)S(1)} %pad_maximum_fusion.1), channel_id=1, source_target_pairs={{0,4},{4,0},{8,12},{12,8},{16,20},{20,16},{24,28},{28,24},{1,5},{5... | collective-permute-start | bytes 3932168 | tf_op jit(solution)/shard_map/ppermute | solution.py:430
  90.7 13.8 %copy-start.26 = (pred[16,128]{1,0:T(8,128)(4,1)S(1)}, pred[16,128]{1,0:T(8,128)(4,1)}, u32[]{:S(2)}) copy-start(pred[16,128]{1,0:T(8,128)(4,1)} %iota_compare_fusion.7) | copy-start | bytes 6148
  104.3 15.5 %copy-start.4 = (bf16[2,1280,128]{2,1,0:T(8,128)(2,1)}, bf16[2,1280,128]{2,1,0:T(8,128)(2,1)S(1)}, u32[]{:S(2)}) copy-start(bf16[2,1280,128]{2,1,0:T(8,128)(2,1)S(1)} %collective-permute-done.13.refs_5_) | copy-start | bytes 1966084
  104.4 15.5 %collective-permute-start.14 = (bf16[256,2560]{1,0:T(8,128)(2,1)S(1)}, bf16[256,2560]{1,0:T(8,128)(2,1)S(1)}, u32[]{:S(2)}, u32[]{:S(2)}) collective-permute-start(bf16[256,2560]{1,0:T(8,128)(2,1)S(1)} %pad_maximum_fusion.2), channel_id=1, source_target_pairs={{0,1},{1,0},{2,3},{3,2},{4,5},{5,4},{6,7},{7,6},{8,9},{9,8},{10,11... | collective-permute-start | bytes 3932168 | tf_op jit(solution)/shard_map/ppermute | solution.py:430
  104.9 15.2 %slice-start.1 = ((s8[8069120]{0:T(1024)(128)(4,1)}), s8[3874816]{0:T(1024)(128)(4,1)S(1)}, s32[]{:S(2)}) async-start(s8[8069120]{0:T(1024)(128)(4,1)} %bitcast.171), calls=%async_computation.1 | async-start | bytes 7749632
  104.9 46.4 %collective-permute-start.23 = (bf16[2,1280,128]{2,1,0:T(8,128)(2,1)}, bf16[2,1280,128]{2,1,0:T(8,128)(2,1)}, u32[]{:S(2)}, u32[]{:S(2)}) collective-permute-start(bf16[2,1280,128]{2,1,0:T(8,128)(2,1)} %get-tuple-element.85), channel_id=1, source_target_pairs={{0,20},{4,16},{8,28},{12,24},{16,4},{20,0},{24,12},{28,8},{1,21},{... | collective-permute-start | bytes 1966088 | tf_op jit(solution)/shard_map/ppermute | solution.py:430
  126.4 4.2 %collective-permute-start.18 = (f32[3,8,16]{2,1,0:T(8,128)S(1)}, f32[3,8,16]{2,1,0:T(8,128)S(1)}, u32[]{:S(2)}, u32[]{:S(2)}) collective-permute-start(f32[3,8,16]{2,1,0:T(8,128)S(1)} %bitcast.188), channel_id=1, source_target_pairs={{0,3},{1,2},{2,1},{3,0},{4,7},{5,6},{6,5},{7,4},{8,11},{9,10},{10,... | collective-permute-start | bytes 4616 | tf_op jit(solution)/shard_map/ppermute | solution.py:430
  126.4 4.2 %collective-permute-start.16 = (f32[3,8,16]{2,1,0:T(8,128)S(1)}, f32[3,8,16]{2,1,0:T(8,128)S(1)}, u32[]{:S(2)}, u32[]{:S(2)}) collective-permute-start(f32[3,8,16]{2,1,0:T(8,128)S(1)} %bitcast.187), channel_id=1, source_target_pairs={{0,1},{1,0},{2,3},{3,2},{4,5},{5,4},{6,7},{7,6},{8,9},{9,8},{10,11... | collective-permute-start | bytes 4616 | tf_op jit(solution)/shard_map/ppermute | solution.py:430
  127.0 34.3 %copy-start.10 = (s32[8]{0:T(128)S(1)}, s32[8]{0:T(128)}, u32[]{:S(2)}) copy-start(s32[8]{0:T(128)} %iota_multiply_fusion.1.start) | copy-start | bytes 100
  127.0 3.7 %collective-permute-start.17 = (f32[3,8,16]{2,1,0:T(8,128)S(1)}, f32[3,8,16]{2,1,0:T(8,128)S(1)}, u32[]{:S(2)}, u32[]{:S(2)}) collective-permute-start(f32[3,8,16]{2,1,0:T(8,128)S(1)} %bitcast.186), channel_id=1, source_target_pairs={{0,2},{1,3},{2,0},{3,1},{4,6},{5,7},{6,4},{7,5},{8,10},{9,11},{10,... | collective-permute-start | bytes 4616 | tf_op jit(solution)/shard_map/ppermute | solution.py:430
  130.6 13.7 %collective-permute-start.20 = (bf16[1,1280,128]{2,1,0:T(8,128)(2,1)}, bf16[1,1280,128]{2,1,0:T(8,128)(2,1)S(1)}, u32[]{:S(2)}, u32[]{:S(2)}) collective-permute-start(bf16[1,1280,128]{2,1,0:T(8,128)(2,1)} %get-tuple-element.115), channel_id=1, source_target_pairs={{0,28},{4,24},{8,20},{12,16},{16,12},{20,8},{24,4},{28,0},{1,29},{... | collective-permute-start | bytes 983048 | tf_op jit(solution)/shard_map/ppermute | solution.py:430
  130.8 20.5 %collective-permute-start.19 = (f32[4,3,16]{2,0,1:T(4,128)S(1)}, f32[4,3,16]{2,0,1:T(4,128)S(1)}, u32[]{:S(2)}, u32[]{:S(2)}) collective-permute-start(f32[4,3,16]{2,0,1:T(4,128)S(1)} %pad_maximum_fusion.13), channel_id=1, source_target_pairs={{0,4},{4,0},{8,12},{12,8},{16,20},{20,16},{24,28},{28,24},{1,5},{5... | collective-permute-start | bytes 2312 | tf_op jit(solution)/shard_map/ppermute | solution.py:430
  133.3 37.4 %collective-permute-start.21 = (bf16[1,1280,128]{2,1,0:T(8,128)(2,1)}, bf16[1,1280,128]{2,1,0:T(8,128)(2,1)S(1)}, u32[]{:S(2)}, u32[]{:S(2)}) collective-permute-start(bf16[1,1280,128]{2,1,0:T(8,128)(2,1)} %get-tuple-element.114), channel_id=1, source_target_pairs={{0,28},{4,24},{8,20},{12,16},{16,12},{20,8},{24,4},{28,0},{1,29},{... | collective-permute-start | bytes 983048 | tf_op jit(solution)/shard_map/ppermute | solution.py:430
  151.4 21.7 %collective-permute-start.24 = (f32[3,16]{1,0:T(4,128)S(1)}, f32[3,16]{1,0:T(4,128)S(1)}, u32[]{:S(2)}, u32[]{:S(2)}) collective-permute-start(f32[3,16]{1,0:T(4,128)S(1)} %bitcast_maximum_fusion.2), channel_id=1, source_target_pairs={{0,8},{4,12},{8,0},{12,4},{16,24},{20,28},{24,16},{28,20},{1,9},{5... | collective-permute-start | bytes 584 | tf_op jit(solution)/shard_map/ppermute | solution.py:430
  158.9 14.2 %collective-permute-start.25 = (f32[3,16]{1,0:T(4,128)S(1)}, f32[3,16]{1,0:T(4,128)S(1)}, u32[]{:S(2)}, u32[]{:S(2)}) collective-permute-start(f32[3,16]{1,0:T(4,128)S(1)} %bitcast_maximum_fusion.1), channel_id=1, source_target_pairs={{0,16},{4,20},{8,24},{12,28},{16,0},{20,4},{24,8},{28,12},{1,17},{... | collective-permute-start | bytes 584 | tf_op jit(solution)/shard_map/ppermute | solution.py:430
  159.0 14.0 %collective-permute-start.26 = (f32[3,16]{1,0:T(4,128)S(1)}, f32[3,16]{1,0:T(4,128)S(1)}, u32[]{:S(2)}, u32[]{:S(2)}) collective-permute-start(f32[3,16]{1,0:T(4,128)S(1)} %bitcast_maximum_fusion), channel_id=1, source_target_pairs={{0,24},{4,28},{8,16},{12,20},{16,8},{20,12},{24,0},{28,4},{1,25},{... | collective-permute-start | bytes 584 | tf_op jit(solution)/shard_map/ppermute | solution.py:430
  (40 other events, 188.0 us)

commit v4 on v3

--- a/solution.py
+++ b/solution.py
@@ -191,10 +191,16 @@
 
     columns = jnp.concatenate(reads + [jnp.zeros((sums.shape[1] - rows, state_dim), f32)], axis=0).T
     column = lax.rem(lax.broadcasted_iota(i32, columns.shape, 1), requests)
-    for k in range(requests):
-        own = jnp.where(column == k, columns, 0.0).astype(bf16)
-        states[k].wait()
-        part = jnp.dot(state_held[k], own, preferred_element_type=f32)
+    for k in range(0, requests, 2):
+        both = range(k, min(k + 2, requests))
+        own = [jnp.where(column == i, columns, 0.0).astype(bf16) for i in both]
+        for i in both:
+            states[i].wait()
+        part = jnp.dot(
+            jnp.concatenate([state_held[i] for i in both], axis=1),
+            jnp.concatenate(own, axis=0),
+            preferred_element_type=f32,
+        )
         if k == 0:
             sums[...] = part
         else:

time: 174 us -> 174 us (level)
  no operation moved by 1% of the time
where the time goes in v4:
time: 174 us
  waiting for transfers between devices  65.2 us (37%)
  starting transfers between devices  35.9 us (21%)
  Pallas kernels  35.5 us (20%)
  local copies, waits for them, and re-layouts  13.9 us (8%)
  other arithmetic  12.2 us (7%)
  matrix products  9.19 us (5%)
  between operations  1.99 us (1%)
    ppermute x27, waiting for transfers between devices, swap(): lax.ppermute(values, axis, [(i, i ^ mask) for i in range(lax.axis_size(ax...  65.2 us
    ppermute x27, starting transfers between devices, swap(): lax.ppermute(values, axis, [(i, i ^ mask) for i in range(lax.axis_size(ax...  35.9 us
    pallas_call x1, Pallas kernels, home_tokens(): pl.pallas_call(functools.partial(home_body, (requests, slots, state_dim,...  13.8 us
    pallas_call x2, Pallas kernels, update_pieces(): pl.pallas_call(functools.partial(update_body, tuple(where), heads), grid_...  9.5 us
    pallas_call x2, Pallas kernels, take_pieces(): pl.pallas_call(functools.partial(pieces_body, tuple(where), size), grid_s...  6.68 us
    pallas_call x1, Pallas kernels, head_logits(): pl.pallas_call(functools.partial(head_body, vocab), grid_spec=pltpu.Prefe...  5.49 us
    unnamed x95, local copies, waits for them, and re-layouts  4.33 us
    dot_general x1, matrix products, project(): jnp.dot(normed, inner_weight, preferred_element_type=f32).astype(bf16)  4.2 us
  transfers between devices with their start and end apart: 27, of which 12 were waited for; matrix products, arithmetic and copies ran while one was open for 15% of the time, Pallas kernels for 20%

profile of v4, /device:TPU:0, one launch (start us, length us, event | category | flops | bytes accessed | tf_op | source)
XLA Modules:
  0.0 173.9 jit_solution(10945144114040054883)
XLA Ops:
  2.9 1.1 fusion.old_inner
  5.2 5.0 %collective-permute-start.2 = (bf16[2,12,2560]{2,1,0:T(8,128)(2,1)S(1)}, bf16[2,12,2560]{2,1,0:T(8,128)(2,1)S(1)}, u32[]{:S(2)}, u32[]{:S(2)}) collective-permute-start(bf16[2,12,2560]{2,1,0:T(8,128)(2,1)S(1)} %get-tuple-element.116), channel_id=1, source_target_pairs={{0,24},{4,28},{8,16},{12,20},{16,8},{20,12},{24,0},{28,4},{1,25},{... | collective-permute-start | bytes 368648 | tf_op jit(solution)/shard_map/ppermute | solution.py:436
  16.1 3.2 %take_pieces.2 = (bf16[4,1280,128]{2,1,0:T(8,128)(2,1)}, bf16[2,1280,128]{2,1,0:T(8,128)(2,1)}) custom-call(s32[16]{0:T(128)} %copy-done.8, s32[8]{0:T(128)} %iota_multiply_fusion.1.start, bf16[16,1280,128]{2,1,0:T(8,128)(2,1)} %bitcast.173), custom_call_target="tpu_custom_call" | custom-call | flops 1 | bytes 1 | tf_op jit(solution)/shard_map/take_pieces/pallas_call | solution.py:53
  21.3 2.8 %collective-permute-done.1 = bf16[2,12,2560]{2,1,0:T(8,128)(2,1)S(1)} collective-permute-done((bf16[2,12,2560]{2,1,0:T(8,128)(2,1)S(1)}, bf16[2,12,2560]{2,1,0:T(8,128)(2,1)S(1)}, u32[]{:S(2)}, u32[]{:S(2)}) %collective-permute-start.1) | collective-permute-done | bytes 122912 | tf_op jit(solution)/shard_map/ppermute | solution.py:436
  24.3 1.6 collective-permute-start.3
  25.9 2.5 %collective-permute-start.22 = (bf16[2,1280,128]{2,1,0:T(8,128)(2,1)}, bf16[2,1280,128]{2,1,0:T(8,128)(2,1)}, u32[]{:S(2)}, u32[]{:S(2)}) collective-permute-start(bf16[2,1280,128]{2,1,0:T(8,128)(2,1)} %get-tuple-element.82), channel_id=1, source_target_pairs={{0,24},{4,28},{8,16},{12,20},{16,8},{20,12},{24,0},{28,4},{1,25},{... | collective-permute-start | bytes 1966088 | tf_op jit(solution)/shard_map/ppermute | solution.py:436
  28.4 4.7 %collective-permute-done.3 = bf16[4,12,2560]{2,1,0:T(8,128)(2,1)S(1)} collective-permute-done((bf16[4,12,2560]{2,1,0:T(8,128)(2,1)S(1)}, bf16[4,12,2560]{2,1,0:T(8,128)(2,1)S(1)}, u32[]{:S(2)}, u32[]{:S(2)}) %collective-permute-start.3) | collective-permute-done | bytes 245792 | tf_op jit(solution)/shard_map/ppermute | solution.py:436
  35.2 13.8 %home_tokens.1 = (bf16[64,2816]{1,0:T(8,128)(2,1)S(1)}, f32[64,2560]{1,0:T(8,128)S(1)}, f32[64,128]{1,0:T(8,128)S(1)}, bf16[64,2560]{1,0:T(8,128)(2,1)S(1)}) custom-call(s32[16]{0:T(128)S(1)} %copy-done.9, bf16[64,2560]{1,0:T(8,128)(2,1)S(1)} %bitcast.169, f32[1,2560]{1,0:T(1,128)S(1)} %broadcast_in_dim.304.norm_gain, ...), custom_call_target="tpu_custom_call" | custom-call | flops 1 | bytes 1 | tf_op jit(solution)/shard_map/home_tokens/pallas_call | solution.py:254
  49.1 1.6 collective-permute-start.6
  57.5 4.2 %convolution_convert_fusion.1 = bf16[64,1280]{1,0:T(8,128)(2,1)S(1)} fusion(bf16[2560,1280]{1,0:T(8,128)(2,1)} %weights_inner.1, bf16[64,2560]{1,0:T(8,128)(2,1)S(1)} %copy-done.12, f32[2560]{0:T(1024)S(1)} %copy-done.25, f32[64]{0:T(128)S(1)} %add_sqrt_fusion), kind=kOutput, calls=%fused_computation.3 | convolution fusion | flops 420167680 | bytes 7055616 | tf_op jit(solution)/shard_map/dot_general | solution.py:522
  61.7 2.3 %collective-permute-start.9 = (bf16[16,2560]{1,0:T(8,128)(2,1)S(1)}, bf16[16,2560]{1,0:T(8,128)(2,1)S(1)}, u32[]{:S(2)}, u32[]{:S(2)}) collective-permute-start(bf16[16,2560]{1,0:T(8,128)(2,1)S(1)} %multiply_convert_fusion), channel_id=1, source_target_pairs={{0,24},{4,28},{8,16},{12,20},{16,8},{20,12},{24,0},{28,4},{1,25},{... | collective-permute-start | bytes 245768 | tf_op jit(solution)/shard_map/ppermute | solution.py:436
  64.1 2.1 %collective-permute-start.7 = (bf16[16,2560]{1,0:T(8,128)(2,1)S(1)}, bf16[16,2560]{1,0:T(8,128)(2,1)S(1)}, u32[]{:S(2)}, u32[]{:S(2)}) collective-permute-start(bf16[16,2560]{1,0:T(8,128)(2,1)S(1)} %multiply_convert_fusion), channel_id=1, source_target_pairs={{0,8},{4,12},{8,0},{12,4},{16,24},{20,28},{24,16},{28,20},{1,9},{5... | collective-permute-start | bytes 245768 | tf_op jit(solution)/shard_map/ppermute | solution.py:436
  69.6 3.5 %take_pieces.3 = (bf16[2,1280,128]{2,1,0:T(8,128)(2,1)}, bf16[2,1280,128]{2,1,0:T(8,128)(2,1)}, bf16[2,1280,128]{2,1,0:T(8,128)(2,1)}, bf16[2,1280,128]{2,1,0:T(8,128)(2,1)}, bf16[2,1280,128]{2,1,0:T(8,128)(2,1)}) custom-call(s32[16]{0:T(128)} %copy-done.8, s32[8]{0:T(128)} %iota_multiply_fusion.1.start, bf16[16,1280,128]{2,1,0:T(8,128)(2,1)} %bitcast.175), custom_call_target="tpu_custom_call" | custom-call | flops 1 | bytes 1 | tf_op jit(solution)/shard_map/take_pieces/pallas_call | solution.py:53
  73.2 2.0 %collective-permute-done.9 = bf16[16,2560]{1,0:T(8,128)(2,1)S(1)} collective-permute-done((bf16[16,2560]{1,0:T(8,128)(2,1)S(1)}, bf16[16,2560]{1,0:T(8,128)(2,1)S(1)}, u32[]{:S(2)}, u32[]{:S(2)}) %collective-permute-start.9) | collective-permute-done | bytes 81952 | tf_op jit(solution)/shard_map/ppermute | solution.py:436
  75.2 2.2 %collective-permute-done.7 = bf16[16,2560]{1,0:T(8,128)(2,1)S(1)} collective-permute-done((bf16[16,2560]{1,0:T(8,128)(2,1)S(1)}, bf16[16,2560]{1,0:T(8,128)(2,1)S(1)}, u32[]{:S(2)}, u32[]{:S(2)}) %collective-permute-start.7) | collective-permute-done | bytes 81952 | tf_op jit(solution)/shard_map/ppermute | solution.py:436
  77.6 9.5 %collective-permute-done.10 = bf16[64,2560]{1,0:T(8,128)(2,1)S(1)} collective-permute-done((bf16[64,2560]{1,0:T(8,128)(2,1)S(1)}, bf16[64,2560]{1,0:T(8,128)(2,1)S(1)}, u32[]{:S(2)}, u32[]{:S(2)}) %collective-permute-start.10) | collective-permute-done | bytes 327712 | tf_op jit(solution)/shard_map/ppermute | solution.py:436
  87.1 1.4 fusion.115
  88.7 1.6 collective-permute-start.12
  90.9 13.6 %collective-permute-done.12 = bf16[128,2560]{1,0:T(8,128)(2,1)S(1)} collective-permute-done((bf16[128,2560]{1,0:T(8,128)(2,1)S(1)}, bf16[128,2560]{1,0:T(8,128)(2,1)S(1)}, u32[]{:S(2)}, u32[]{:S(2)}) %collective-permute-start.12) | collective-permute-done | bytes 655392 | tf_op jit(solution)/shard_map/ppermute | solution.py:436
  105.2 14.8 %collective-permute-done.15 = bf16[4,1280,128]{2,1,0:T(8,128)(2,1)S(1)} collective-permute-done((bf16[4,1280,128]{2,1,0:T(8,128)(2,1)S(1)}, bf16[4,1280,128]{2,1,0:T(8,128)(2,1)S(1)}, u32[]{:S(2)}, u32[]{:S(2)}) %collective-permute-start.15) | collective-permute-done | bytes 1310752 | tf_op jit(solution)/shard_map/ppermute | solution.py:436
  120.4 5.5 %head_logits.1 = (f32[1,512]{1,0:T(1,128)S(1)}, f32[1,512]{1,0:T(1,128)S(1)}) custom-call(s32[1]{0:T(128)} %bitcast.38.first, s32[1,512]{1,0:T(1,128)S(1)} %bitcast.170, bf16[512,2560]{1,0:T(8,128)(2,1)S(1)} %pad_maximum_fusion.final, bf16[1572,2560]{1,0:T(8,128)(2,1)S(1)} %bitcast.172), custom_call_target="tpu_custom_call" | custom-call | flops 4120903680 | bytes 8048640 | tf_op jit(solution)/shard_map/head_logits/pallas_call | solution.py:372
  127.3 1.5 collective-permute-start.17
  128.8 2.0 %fusion.117 = (bf16[1,1280,128]{2,1,0:T(8,128)(2,1)}, bf16[1,1280,128]{2,1,0:T(8,128)(2,1)}) fusion(bf16[2,1280,128]{2,1,0:T(8,128)(2,1)} %get-tuple-element.77), kind=kLoop, calls=%fused_computation.305 | loop fusion | bytes 1310720 | tf_op jit(solution)/shard_map/slice | solution.py:620
  131.0 1.2 collective-permute-start.19
  133.3 4.1 %collective-permute-start.21 = (bf16[1,1280,128]{2,1,0:T(8,128)(2,1)}, bf16[1,1280,128]{2,1,0:T(8,128)(2,1)S(1)}, u32[]{:S(2)}, u32[]{:S(2)}) collective-permute-start(bf16[1,1280,128]{2,1,0:T(8,128)(2,1)} %get-tuple-element.114), channel_id=1, source_target_pairs={{0,28},{4,24},{8,20},{12,16},{16,12},{20,8},{24,4},{28,0},{1,29},{... | collective-permute-start | bytes 983048 | tf_op jit(solution)/shard_map/ppermute | solution.py:436
  137.4 7.1 %collective-permute-done.20.refs_0_ = bf16[1,1280,128]{2,1,0:T(8,128)(2,1)S(1)} collective-permute-done((bf16[1,1280,128]{2,1,0:T(8,128)(2,1)}, bf16[1,1280,128]{2,1,0:T(8,128)(2,1)S(1)}, u32[]{:S(2)}, u32[]{:S(2)}) %collective-permute-start.20) | collective-permute-done | bytes 327712 | tf_op jit(solution)/shard_map/ppermute | solution.py:436
  144.5 7.0 %collective-permute-done.19 = f32[4,3,16]{2,0,1:T(4,128)S(1)} collective-permute-done((f32[4,3,16]{2,0,1:T(4,128)S(1)}, f32[4,3,16]{2,0,1:T(4,128)S(1)}, u32[]{:S(2)}, u32[]{:S(2)}) %collective-permute-start.19) | collective-permute-done | bytes 800 | tf_op jit(solution)/shard_map/ppermute | solution.py:436
  151.6 7.5 %collective-permute-start.24 = (f32[3,16]{1,0:T(4,128)S(1)}, f32[3,16]{1,0:T(4,128)S(1)}, u32[]{:S(2)}, u32[]{:S(2)}) collective-permute-start(f32[3,16]{1,0:T(4,128)S(1)} %bitcast_maximum_fusion.2), channel_id=1, source_target_pairs={{0,8},{4,12},{8,0},{12,4},{16,24},{20,28},{24,16},{28,20},{1,9},{5... | collective-permute-start | bytes 584 | tf_op jit(solution)/shard_map/ppermute | solution.py:436
  159.3 2.3 %collective-permute-start.26 = (f32[3,16]{1,0:T(4,128)S(1)}, f32[3,16]{1,0:T(4,128)S(1)}, u32[]{:S(2)}, u32[]{:S(2)}) collective-permute-start(f32[3,16]{1,0:T(4,128)S(1)} %bitcast_maximum_fusion), channel_id=1, source_target_pairs={{0,24},{4,28},{8,16},{12,20},{16,8},{20,12},{24,0},{28,4},{1,25},{... | collective-permute-start | bytes 584 | tf_op jit(solution)/shard_map/ppermute | solution.py:436
  161.6 1.1 copy-done.3
  163.7 7.1 %update_pieces.2.refs_2_ = bf16[16,1280,128]{2,1,0:T(8,128)(2,1)} custom-call(s32[16]{0:T(128)S(1)} %get-tuple-element.93.target, s32[8]{0:T(128)S(1)} %copy-done.10, f32[16,20]{1,0:T(8,128)S(1)} %get-tuple-element.153.keep, bf16[1280,128]{1,0:T(8,128)(2,1)S(1)} %bitcast.167, bf16[16,128,128]{2,1,0:T(8,128)(2,1)S(1)} %broadcast_select_fusion.writes, ...), custom_call_target="tpu_custom_call" | custom-call | tf_op jit(solution)/shard_map/update_pieces/pallas_call | solution.py:322
  170.9 2.4 %update_pieces.3 = bf16[16,1280,128]{2,1,0:T(8,128)(2,1)} custom-call(s32[16]{0:T(128)S(1)} %get-tuple-element.93.target, s32[8]{0:T(128)S(1)} %copy-done.10, f32[16,20]{1,0:T(8,128)S(1)} %get-tuple-element.153.keep, bf16[1280,128]{1,0:T(8,128)(2,1)S(1)} %bitcast.168, ...), custom_call_target="tpu_custom_call", output_to_operand_aliasing={{}: (7, {})} | custom-call | tf_op jit(solution)/shard_map/update_pieces/pallas_call | solution.py:322
  (256 shorter events, 29.5 us)
Async XLA Ops:
  5.2 16.1 %collective-permute-start.2 = (bf16[2,12,2560]{2,1,0:T(8,128)(2,1)S(1)}, bf16[2,12,2560]{2,1,0:T(8,128)(2,1)S(1)}, u32[]{:S(2)}, u32[]{:S(2)}) collective-permute-start(bf16[2,12,2560]{2,1,0:T(8,128)(2,1)S(1)} %get-tuple-element.116), channel_id=1, source_target_pairs={{0,24},{4,28},{8,16},{12,20},{16,8},{20,12},{24,0},{28,4},{1,25},{... | collective-permute-start | bytes 368648 | tf_op jit(solution)/shard_map/ppermute | solution.py:436
  10.3 13.9 %collective-permute-start.1 = (bf16[2,12,2560]{2,1,0:T(8,128)(2,1)S(1)}, bf16[2,12,2560]{2,1,0:T(8,128)(2,1)S(1)}, u32[]{:S(2)}, u32[]{:S(2)}) collective-permute-start(bf16[2,12,2560]{2,1,0:T(8,128)(2,1)S(1)} %get-tuple-element.117), channel_id=1, source_target_pairs={{0,16},{4,20},{8,24},{12,28},{16,0},{20,4},{24,8},{28,12},{1,17},{... | collective-permute-start | bytes 368648 | tf_op jit(solution)/shard_map/ppermute | solution.py:436
  10.3 13.9 %collective-permute-start = (bf16[2,12,2560]{2,1,0:T(8,128)(2,1)S(1)}, bf16[2,12,2560]{2,1,0:T(8,128)(2,1)S(1)}, u32[]{:S(2)}, u32[]{:S(2)}) collective-permute-start(bf16[2,12,2560]{2,1,0:T(8,128)(2,1)S(1)} %get-tuple-element.118), channel_id=1, source_target_pairs={{0,8},{4,12},{8,0},{12,4},{16,24},{20,28},{24,16},{28,20},{1,9},{5... | collective-permute-start | bytes 368648 | tf_op jit(solution)/shard_map/ppermute | solution.py:436
  24.3 8.8 %collective-permute-start.3 = (bf16[4,12,2560]{2,1,0:T(8,128)(2,1)S(1)}, bf16[4,12,2560]{2,1,0:T(8,128)(2,1)S(1)}, u32[]{:S(2)}, u32[]{:S(2)}) collective-permute-start(bf16[4,12,2560]{2,1,0:T(8,128)(2,1)S(1)} %pad_maximum_fusion.4), channel_id=1, source_target_pairs={{0,4},{4,0},{8,12},{12,8},{16,20},{20,16},{24,28},{28,24},{1,5},{5... | collective-permute-start | bytes 737288 | tf_op jit(solution)/shard_map/ppermute | solution.py:436
  25.9 135.7 %collective-permute-start.22 = (bf16[2,1280,128]{2,1,0:T(8,128)(2,1)}, bf16[2,1280,128]{2,1,0:T(8,128)(2,1)}, u32[]{:S(2)}, u32[]{:S(2)}) collective-permute-start(bf16[2,1280,128]{2,1,0:T(8,128)(2,1)} %get-tuple-element.82), channel_id=1, source_target_pairs={{0,24},{4,28},{8,16},{12,20},{16,8},{20,12},{24,0},{28,4},{1,25},{... | collective-permute-start | bytes 1966088 | tf_op jit(solution)/shard_map/ppermute | solution.py:436
  28.4 58.7 %collective-permute-start.11 = (bf16[4,1280,128]{2,1,0:T(8,128)(2,1)}, bf16[4,1280,128]{2,1,0:T(8,128)(2,1)}, u32[]{:S(2)}, u32[]{:S(2)}) collective-permute-start(bf16[4,1280,128]{2,1,0:T(8,128)(2,1)} %get-tuple-element.64), channel_id=1, source_target_pairs={{0,8},{4,12},{8,0},{12,4},{16,24},{20,28},{24,16},{28,20},{1,9},{5... | collective-permute-start | bytes 3932168 | tf_op jit(solution)/shard_map/ppermute | solution.py:436
  49.1 4.1 %collective-permute-start.4 = (bf16[16,2816]{1,0:T(8,128)(2,1)S(1)}, bf16[16,2816]{1,0:T(8,128)(2,1)}, u32[]{:S(2)}, u32[]{:S(2)}) collective-permute-start(bf16[16,2816]{1,0:T(8,128)(2,1)S(1)} %get-tuple-element.124), channel_id=1, source_target_pairs={{0,1},{1,0},{2,3},{3,2},{4,5},{5,4},{6,7},{7,6},{8,9},{9,8},{10,11... | collective-permute-start | bytes 270344 | tf_op jit(solution)/shard_map/ppermute | solution.py:436
  49.1 4.9 %collective-permute-start.6 = (bf16[16,2816]{1,0:T(8,128)(2,1)S(1)}, bf16[16,2816]{1,0:T(8,128)(2,1)}, u32[]{:S(2)}, u32[]{:S(2)}) collective-permute-start(bf16[16,2816]{1,0:T(8,128)(2,1)S(1)} %get-tuple-element.125), channel_id=1, source_target_pairs={{0,3},{1,2},{2,1},{3,0},{4,7},{5,6},{6,5},{7,4},{8,11},{9,10},{10,... | collective-permute-start | bytes 270344 | tf_op jit(solution)/shard_map/ppermute | solution.py:436
  50.8 5.3 %collective-permute-start.5 = (bf16[16,2816]{1,0:T(8,128)(2,1)S(1)}, bf16[16,2816]{1,0:T(8,128)(2,1)S(1)}, u32[]{:S(2)}, u32[]{:S(2)}) collective-permute-start(bf16[16,2816]{1,0:T(8,128)(2,1)S(1)} %get-tuple-element.126), channel_id=1, source_target_pairs={{0,2},{1,3},{2,0},{3,1},{4,6},{5,7},{6,4},{7,5},{8,10},{9,11},{10,... | collective-permute-start | bytes 270344 | tf_op jit(solution)/shard_map/ppermute | solution.py:436
  61.7 13.5 %collective-permute-start.9 = (bf16[16,2560]{1,0:T(8,128)(2,1)S(1)}, bf16[16,2560]{1,0:T(8,128)(2,1)S(1)}, u32[]{:S(2)}, u32[]{:S(2)}) collective-permute-start(bf16[16,2560]{1,0:T(8,128)(2,1)S(1)} %multiply_convert_fusion), channel_id=1, source_target_pairs={{0,24},{4,28},{8,16},{12,20},{16,8},{20,12},{24,0},{28,4},{1,25},{... | collective-permute-start | bytes 245768 | tf_op jit(solution)/shard_map/ppermute | solution.py:436
  64.0 11.2 %collective-permute-start.8 = (bf16[16,2560]{1,0:T(8,128)(2,1)S(1)}, bf16[16,2560]{1,0:T(8,128)(2,1)S(1)}, u32[]{:S(2)}, u32[]{:S(2)}) collective-permute-start(bf16[16,2560]{1,0:T(8,128)(2,1)S(1)} %multiply_convert_fusion), channel_id=1, source_target_pairs={{0,16},{4,20},{8,24},{12,28},{16,0},{20,4},{24,8},{28,12},{1,17},{... | collective-permute-start | bytes 245768 | tf_op jit(solution)/shard_map/ppermute | solution.py:436
  64.1 13.4 %collective-permute-start.7 = (bf16[16,2560]{1,0:T(8,128)(2,1)S(1)}, bf16[16,2560]{1,0:T(8,128)(2,1)S(1)}, u32[]{:S(2)}, u32[]{:S(2)}) collective-permute-start(bf16[16,2560]{1,0:T(8,128)(2,1)S(1)} %multiply_convert_fusion), channel_id=1, source_target_pairs={{0,8},{4,12},{8,0},{12,4},{16,24},{20,28},{24,16},{28,20},{1,9},{5... | collective-permute-start | bytes 245768 | tf_op jit(solution)/shard_map/ppermute | solution.py:436
  75.2 29.4 %collective-permute-start.13 = (bf16[2,1280,128]{2,1,0:T(8,128)(2,1)}, bf16[2,1280,128]{2,1,0:T(8,128)(2,1)S(1)}, u32[]{:S(2)}, u32[]{:S(2)}) collective-permute-start(bf16[2,1280,128]{2,1,0:T(8,128)(2,1)} %get-tuple-element.70), channel_id=1, source_target_pairs={{0,16},{4,20},{8,24},{12,28},{16,0},{20,4},{24,8},{28,12},{1,17},{... | collective-permute-start | bytes 1966088 | tf_op jit(solution)/shard_map/ppermute | solution.py:436
  77.5 9.6 %collective-permute-start.10 = (bf16[64,2560]{1,0:T(8,128)(2,1)S(1)}, bf16[64,2560]{1,0:T(8,128)(2,1)S(1)}, u32[]{:S(2)}, u32[]{:S(2)}) collective-permute-start(bf16[64,2560]{1,0:T(8,128)(2,1)S(1)} %pad_maximum_fusion.7), channel_id=1, source_target_pairs={{0,4},{4,0},{8,12},{12,8},{16,20},{20,16},{24,28},{28,24},{1,5},{5... | collective-permute-start | bytes 983048 | tf_op jit(solution)/shard_map/ppermute | solution.py:436
  88.6 31.7 %slice-start = ((s8[8069120]{0:T(1024)(128)(4,1)}), s8[4194304]{0:T(1024)(128)(4,1)S(1)}, s32[]{:S(2)}) async-start(s8[8069120]{0:T(1024)(128)(4,1)} %bitcast.171), calls=%async_computation | async-start | bytes 8388608
  88.7 15.8 %collective-permute-start.12 = (bf16[128,2560]{1,0:T(8,128)(2,1)S(1)}, bf16[128,2560]{1,0:T(8,128)(2,1)S(1)}, u32[]{:S(2)}, u32[]{:S(2)}) collective-permute-start(bf16[128,2560]{1,0:T(8,128)(2,1)S(1)} %constant_dynamic-update-slice_fusion), channel_id=1, source_target_pairs={{0,2},{1,3},{2,0},{3,1},{4,6},{5,7},{6,4},{7,5},{8,10},{9,11},{10,... | collective-permute-start | bytes 1966088 | tf_op jit(solution)/shard_map/ppermute | solution.py:436
  90.4 29.6 %collective-permute-start.15 = (bf16[4,1280,128]{2,1,0:T(8,128)(2,1)S(1)}, bf16[4,1280,128]{2,1,0:T(8,128)(2,1)S(1)}, u32[]{:S(2)}, u32[]{:S(2)}) collective-permute-start(bf16[4,1280,128]{2,1,0:T(8,128)(2,1)S(1)} %pad_maximum_fusion.1), channel_id=1, source_target_pairs={{0,4},{4,0},{8,12},{12,8},{16,20},{20,16},{24,28},{28,24},{1,5},{5... | collective-permute-start | bytes 3932168 | tf_op jit(solution)/shard_map/ppermute | solution.py:436
  90.9 13.9 %copy-start.26 = (pred[16,128]{1,0:T(8,128)(4,1)S(1)}, pred[16,128]{1,0:T(8,128)(4,1)}, u32[]{:S(2)}) copy-start(pred[16,128]{1,0:T(8,128)(4,1)} %iota_compare_fusion.7) | copy-start | bytes 6148
  104.6 15.5 %copy-start.4 = (bf16[2,1280,128]{2,1,0:T(8,128)(2,1)}, bf16[2,1280,128]{2,1,0:T(8,128)(2,1)S(1)}, u32[]{:S(2)}) copy-start(bf16[2,1280,128]{2,1,0:T(8,128)(2,1)S(1)} %collective-permute-done.13.refs_5_) | copy-start | bytes 1966084
  104.6 15.5 %collective-permute-start.14 = (bf16[256,2560]{1,0:T(8,128)(2,1)S(1)}, bf16[256,2560]{1,0:T(8,128)(2,1)S(1)}, u32[]{:S(2)}, u32[]{:S(2)}) collective-permute-start(bf16[256,2560]{1,0:T(8,128)(2,1)S(1)} %pad_maximum_fusion.2), channel_id=1, source_target_pairs={{0,1},{1,0},{2,3},{3,2},{4,5},{5,4},{6,7},{7,6},{8,9},{9,8},{10,11... | collective-permute-start | bytes 3932168 | tf_op jit(solution)/shard_map/ppermute | solution.py:436
  105.1 15.2 %slice-start.1 = ((s8[8069120]{0:T(1024)(128)(4,1)}), s8[3874816]{0:T(1024)(128)(4,1)S(1)}, s32[]{:S(2)}) async-start(s8[8069120]{0:T(1024)(128)(4,1)} %bitcast.171), calls=%async_computation.1 | async-start | bytes 7749632
  105.2 46.4 %collective-permute-start.23 = (bf16[2,1280,128]{2,1,0:T(8,128)(2,1)}, bf16[2,1280,128]{2,1,0:T(8,128)(2,1)}, u32[]{:S(2)}, u32[]{:S(2)}) collective-permute-start(bf16[2,1280,128]{2,1,0:T(8,128)(2,1)} %get-tuple-element.85), channel_id=1, source_target_pairs={{0,20},{4,16},{8,28},{12,24},{16,4},{20,0},{24,12},{28,8},{1,21},{... | collective-permute-start | bytes 1966088 | tf_op jit(solution)/shard_map/ppermute | solution.py:436
  126.6 4.2 %collective-permute-start.18 = (f32[3,8,16]{2,1,0:T(8,128)S(1)}, f32[3,8,16]{2,1,0:T(8,128)S(1)}, u32[]{:S(2)}, u32[]{:S(2)}) collective-permute-start(f32[3,8,16]{2,1,0:T(8,128)S(1)} %bitcast.188), channel_id=1, source_target_pairs={{0,3},{1,2},{2,1},{3,0},{4,7},{5,6},{6,5},{7,4},{8,11},{9,10},{10,... | collective-permute-start | bytes 4616 | tf_op jit(solution)/shard_map/ppermute | solution.py:436
  126.7 4.1 %collective-permute-start.16 = (f32[3,8,16]{2,1,0:T(8,128)S(1)}, f32[3,8,16]{2,1,0:T(8,128)S(1)}, u32[]{:S(2)}, u32[]{:S(2)}) collective-permute-start(f32[3,8,16]{2,1,0:T(8,128)S(1)} %bitcast.187), channel_id=1, source_target_pairs={{0,1},{1,0},{2,3},{3,2},{4,5},{5,4},{6,7},{7,6},{8,9},{9,8},{10,11... | collective-permute-start | bytes 4616 | tf_op jit(solution)/shard_map/ppermute | solution.py:436
  127.3 34.3 %copy-start.10 = (s32[8]{0:T(128)S(1)}, s32[8]{0:T(128)}, u32[]{:S(2)}) copy-start(s32[8]{0:T(128)} %iota_multiply_fusion.1.start) | copy-start | bytes 100
  127.3 3.7 %collective-permute-start.17 = (f32[3,8,16]{2,1,0:T(8,128)S(1)}, f32[3,8,16]{2,1,0:T(8,128)S(1)}, u32[]{:S(2)}, u32[]{:S(2)}) collective-permute-start(f32[3,8,16]{2,1,0:T(8,128)S(1)} %bitcast.186), channel_id=1, source_target_pairs={{0,2},{1,3},{2,0},{3,1},{4,6},{5,7},{6,4},{7,5},{8,10},{9,11},{10,... | collective-permute-start | bytes 4616 | tf_op jit(solution)/shard_map/ppermute | solution.py:436
  130.8 13.7 %collective-permute-start.20 = (bf16[1,1280,128]{2,1,0:T(8,128)(2,1)}, bf16[1,1280,128]{2,1,0:T(8,128)(2,1)S(1)}, u32[]{:S(2)}, u32[]{:S(2)}) collective-permute-start(bf16[1,1280,128]{2,1,0:T(8,128)(2,1)} %get-tuple-element.115), channel_id=1, source_target_pairs={{0,28},{4,24},{8,20},{12,16},{16,12},{20,8},{24,4},{28,0},{1,29},{... | collective-permute-start | bytes 983048 | tf_op jit(solution)/shard_map/ppermute | solution.py:436
  131.0 20.5 %collective-permute-start.19 = (f32[4,3,16]{2,0,1:T(4,128)S(1)}, f32[4,3,16]{2,0,1:T(4,128)S(1)}, u32[]{:S(2)}, u32[]{:S(2)}) collective-permute-start(f32[4,3,16]{2,0,1:T(4,128)S(1)} %pad_maximum_fusion.13), channel_id=1, source_target_pairs={{0,4},{4,0},{8,12},{12,8},{16,20},{20,16},{24,28},{28,24},{1,5},{5... | collective-permute-start | bytes 2312 | tf_op jit(solution)/shard_map/ppermute | solution.py:436
  133.3 37.6 %collective-permute-start.21 = (bf16[1,1280,128]{2,1,0:T(8,128)(2,1)}, bf16[1,1280,128]{2,1,0:T(8,128)(2,1)S(1)}, u32[]{:S(2)}, u32[]{:S(2)}) collective-permute-start(bf16[1,1280,128]{2,1,0:T(8,128)(2,1)} %get-tuple-element.114), channel_id=1, source_target_pairs={{0,28},{4,24},{8,20},{12,16},{16,12},{20,8},{24,4},{28,0},{1,29},{... | collective-permute-start | bytes 983048 | tf_op jit(solution)/shard_map/ppermute | solution.py:436
  151.6 21.7 %collective-permute-start.24 = (f32[3,16]{1,0:T(4,128)S(1)}, f32[3,16]{1,0:T(4,128)S(1)}, u32[]{:S(2)}, u32[]{:S(2)}) collective-permute-start(f32[3,16]{1,0:T(4,128)S(1)} %bitcast_maximum_fusion.2), channel_id=1, source_target_pairs={{0,8},{4,12},{8,0},{12,4},{16,24},{20,28},{24,16},{28,20},{1,9},{5... | collective-permute-start | bytes 584 | tf_op jit(solution)/shard_map/ppermute | solution.py:436
  159.1 14.2 %collective-permute-start.25 = (f32[3,16]{1,0:T(4,128)S(1)}, f32[3,16]{1,0:T(4,128)S(1)}, u32[]{:S(2)}, u32[]{:S(2)}) collective-permute-start(f32[3,16]{1,0:T(4,128)S(1)} %bitcast_maximum_fusion.1), channel_id=1, source_target_pairs={{0,16},{4,20},{8,24},{12,28},{16,0},{20,4},{24,8},{28,12},{1,17},{... | collective-permute-start | bytes 584 | tf_op jit(solution)/shard_map/ppermute | solution.py:436
  159.3 14.0 %collective-permute-start.26 = (f32[3,16]{1,0:T(4,128)S(1)}, f32[3,16]{1,0:T(4,128)S(1)}, u32[]{:S(2)}, u32[]{:S(2)}) collective-permute-start(f32[3,16]{1,0:T(4,128)S(1)} %bitcast_maximum_fusion), channel_id=1, source_target_pairs={{0,24},{4,28},{8,16},{12,20},{16,8},{20,12},{24,0},{28,4},{1,25},{... | collective-permute-start | bytes 584 | tf_op jit(solution)/shard_map/ppermute | solution.py:436
  (40 other events, 187.8 us)
